TPU v7x, 128 devices: a whole 4x4x4 slice. The times are simulated.
128 devices in a mesh: cell: 4 (over x), energy: 32 (over y, z, core).
Axes of the slice: x: 4, y: 4, z: 4, core: 2. Of those that a mesh axis runs over, the one named last changes fastest.
Arguments:
- hamiltonian: float32 [4, 2, 128, 128], P('cell'), may hold values from -2 to 2, as said below
- coupling: float32 [4, 2, 128, 128], P('cell'), may hold values from -0.25 to 0.25
- sigma_in: float32 [4, 128, 2, 128, 128], P('cell', 'energy'), may hold values from -1 to 1, as said below
- mode_offsets: int32 [4], replicated, may hold values from 1 to 8, as said below
- mode_coupling: float32 [4], replicated, may hold values from 0.1 to 0.4
- energy_owner: int32 [128], replicated, may hold values from 0 to 127, as said below
Outputs:
- green_diag: float32 [4, 128, 2, 128, 128], P('cell', 'energy')
- sigma_out: float32 [4, 128, 2, 128, 128], P('cell', 'energy')
Inputs may be any that keep to these rules, and one draw needn't show every extreme that they name: `hamiltonian`: every block is Hermitian. `sigma_in`: the anti-Hermitian part of every block is negative semidefinite. `energy_owner`: every energy index stands in exactly one slot; slot s holds an index from 4 * (s // 4) to 4 * (s // 4) + 3. `mode_offsets`: some mode has offset exactly 8.
All inputs are finite; a program needn't handle non-finite values.
Results may differ from a plain program's by a relative error of at most 0.00011.
Values sent between devices are 32-bit elements; how exact they have to be, the bound alone decides.
A program may use at most 64 MiB of HBM per device.

v0:
```python
import jax
import jax.numpy as jnp
from jax import lax
from jax.sharding import PartitionSpec as P

OFFSET_MAX = 8


PRECISE = lax.Precision.HIGHEST
BROADENING = 0.2
CONTACT_RATE = 0.5
LEAD_WIDTH = 1.0
BAND_LOW = -2.5
BAND_SPAN = 5.0


def from_behind(block, axis, distance):
    devices = range(lax.axis_size(axis))
    route = [(i - distance, i) for i in devices if i - distance in devices]
    return lax.ppermute(block, axis, route)


def complex_product(first, second):
    first_real, first_imag = (first[..., 0, :, :], first[..., 1, :, :])
    second_real, second_imag = (second[..., 0, :, :], second[..., 1, :, :])
    real_part = jnp.matmul(first_real, second_real, precision=PRECISE) - jnp.matmul(
        first_imag, second_imag, precision=PRECISE
    )
    imag_part = jnp.matmul(first_real, second_imag, precision=PRECISE) + jnp.matmul(
        first_imag, second_real, precision=PRECISE
    )
    return jnp.stack([real_part, imag_part], axis=-3)


def adjoint(matrix):
    return jnp.stack(
        [jnp.swapaxes(matrix[..., 0, :, :], -1, -2), -jnp.swapaxes(matrix[..., 1, :, :], -1, -2)],
        axis=-3,
    )


def invert(matrix):
    orbitals = matrix.shape[-1]
    gram_matrix = complex_product(adjoint(matrix), matrix)
    gram_real, gram_imag = (gram_matrix[..., 0, :, :], gram_matrix[..., 1, :, :])
    embedded = jnp.concatenate(
        [jnp.concatenate([gram_real, -gram_imag], -1), jnp.concatenate([gram_imag, gram_real], -1)],
        -2,
    )
    factor_low = jnp.linalg.cholesky(embedded)
    right_side = jnp.concatenate(
        [jnp.swapaxes(matrix[..., 0, :, :], -1, -2), -jnp.swapaxes(matrix[..., 1, :, :], -1, -2)],
        -2,
    )
    halfway = lax.linalg.triangular_solve(factor_low, right_side, left_side=True, lower=True)
    solution = lax.linalg.triangular_solve(
        factor_low, halfway, left_side=True, lower=True, transpose_a=True
    )
    return jnp.stack([solution[..., :orbitals, :], solution[..., orbitals:, :]], axis=-3)


def left_sweep(local_shifted, entering, links):

    def left_advance(schur_term, inputs):
        cell_block, cell_link = inputs
        partial_green = invert(cell_block - schur_term)
        next_term = complex_product(adjoint(cell_link), complex_product(partial_green, cell_link))
        return (next_term, schur_term)

    outgoing, collected = lax.scan(left_advance, entering, (local_shifted, links))
    return (collected, outgoing)


def right_sweep(local_shifted, beyond, links):

    def right_advance(partial_green, inputs):
        cell_block, cell_link = inputs
        schur_term = complex_product(cell_link, complex_product(partial_green, adjoint(cell_link)))
        next_green = invert(cell_block - schur_term)
        return (next_green, schur_term)

    first_green, collected = lax.scan(right_advance, beyond, (local_shifted, links), reverse=True)
    return (collected, first_green)


def per_device(hamiltonian, coupling, sigma_in, mode_offsets, mode_coupling, energy_owner):
    slot_count = sigma_in.shape[1]
    orbitals = hamiltonian.shape[-1]
    chain_length = lax.axis_size("cell")
    energy_devices = lax.axis_size("energy")
    chain_index = lax.axis_index("cell")
    energy_index = lax.axis_index("energy")
    energy_count = slot_count * energy_devices
    identity = jnp.eye(orbitals, dtype=jnp.float32)
    nothing = jnp.zeros_like(identity)
    contact = jnp.stack([nothing, -CONTACT_RATE * identity])
    lead_green = jnp.stack([nothing, -LEAD_WIDTH * identity])
    at_start = (chain_index == 0).astype(jnp.float32)
    at_end = chain_index == chain_length - 1
    my_owner = lax.dynamic_slice_in_dim(energy_owner, energy_index * slot_count, slot_count)
    energy_level = BAND_LOW + BAND_SPAN * my_owner.astype(jnp.float32) / (energy_count - 1)
    broadened = jnp.broadcast_to(BROADENING * identity, (slot_count, orbitals, orbitals))
    diagonal_part = jnp.stack([energy_level[:, None, None] * identity, broadened], axis=1)
    shifted = diagonal_part[None] - hamiltonian[:, None] - sigma_in
    start_zeros = jnp.zeros((slot_count, 2, orbitals, orbitals), jnp.float32)

    def left_round(unused_index, received):
        unused_terms, outgoing = left_sweep(shifted, received + contact * at_start, coupling)
        return from_behind(outgoing, "cell", 1)

    received = lax.fori_loop(0, chain_length - 1, left_round, start_zeros)
    left_terms, unused_left = left_sweep(shifted, received + contact * at_start, coupling)

    def right_round(unused_index, beyond):
        unused_terms, first_green = right_sweep(
            shifted, jnp.where(at_end, lead_green, beyond), coupling
        )
        return from_behind(first_green, "cell", -1)

    beyond = lax.fori_loop(0, chain_length - 1, right_round, start_zeros)
    right_terms, unused_right = right_sweep(
        shifted, jnp.where(at_end, lead_green, beyond), coupling
    )
    green_diag = invert(shifted - left_terms - right_terms)

    def weight_rows(source_owner):
        offset_table = source_owner[None, :] - my_owner[:, None]
        matches = (offset_table[:, :, None] == -mode_offsets).astype(jnp.float32) + (
            offset_table[:, :, None] == mode_offsets
        ).astype(jnp.float32)
        return jnp.sum(matches * mode_coupling, -1)

    def contribute(running_sum, blocks, device_offset):
        first_slot = jnp.clip(
            (energy_index - device_offset) * slot_count, 0, energy_count - slot_count
        )
        source_owner = lax.dynamic_slice_in_dim(energy_owner, first_slot, slot_count)
        weights = weight_rows(source_owner)
        return running_sum + jnp.einsum("sk,ckrij->csrij", weights, blocks, precision=PRECISE)

    reach = min(-(-OFFSET_MAX // slot_count), energy_devices - 1)
    sigma_out = contribute(jnp.zeros_like(green_diag), green_diag, 0)
    for distance in range(1, reach + 1):
        for direction in (1, -1):
            arrived = from_behind(green_diag, "energy", direction * distance)
            sigma_out = contribute(sigma_out, arrived, direction * distance)
    return (green_diag, sigma_out)


def solution(mesh):
    in_specs = (
        P("cell", None, None, None),
        P("cell", None, None, None),
        P("cell", "energy", None, None, None),
        P(),
        P(),
        P(),
    )
    out_specs = (P("cell", "energy", None, None, None), P("cell", "energy", None, None, None))
    return jax.shard_map(
        per_device, mesh=mesh, in_specs=in_specs, out_specs=out_specs, check_vma=False
    )
```

profile of v0, /device:TPU:25, one launch (start us, length us, event | category | flops | bytes accessed | tf_op | source)
XLA Modules:
  0.0 1821.9 jit_solution(11183352796262908051)
XLA Ops:
  7.6 773.2 %while.54 = (s32[]{:T(128)}, f32[4,2,128,128]{3,2,0,1:T(8,128)S(1)}, f32[1,4,2,128,128]{3,4,1,2,0:T(8,128)S(1)}, pred[]{:T(512)}, f32[2,128,128]{2,1,0:T(8,128)}...) while((s32[]{:T(128)}, ...), condition=%wide.region_7.11_spmd, body=%wide.region_6.10_spmd.sunk | while | flops 2017952768 | bytes 36841456 | solution.py:120
  22.1 46.9 %custom-call.71 = f32[4,128,128]{2,1,0:T(8,128)S(1)} custom-call(f32[4,128,128]{2,1,0:T(8,128)S(1)} %cholesky.566), custom_call_target="Cholesky" | custom-call | tf_op jit(solution)/shard_map/while/body/eval_jaxpr/while/body/eval_jaxpr/jit(cholesky)/cholesky | solution.py:50
  70.5 40.8 %custom-call.72 = f32[4,1,128,128]{2,3,1,0:T(8,128)} custom-call(f32[4,1,128,128]{3,2,1,0:T(8,128)} %select_bitcast_fusion.6), custom_call_target="InvertDiagBlocksLowerTriangular" | custom-call | tf_op jit(solution)/shard_map/while/body/eval_jaxpr/while/body/eval_jaxpr/jit(cholesky)/cholesky | solution.py:50
  113.9 47.7 %custom-call.73 = f32[4,128,128]{2,1,0:T(8,128)S(1)} custom-call(f32[4,128,128]{2,1,0:T(8,128)} %convolution_subtract_fusion.33), custom_call_target="Cholesky" | custom-call | tf_op jit(solution)/shard_map/while/body/eval_jaxpr/while/body/eval_jaxpr/jit(cholesky)/cholesky | solution.py:50
  163.2 5.6 while.57
  163.9 2.1 bitcast_dynamic-update-slice_fusion.8
  166.7 2.1 bitcast_dynamic-update-slice_fusion.8
  168.8 79.4 %custom-call.75 = f32[4,2,128,128]{2,3,1,0:T(8,128)S(1)} custom-call(f32[4,2,128,128]{3,2,1,0:T(8,128)} %bitcast.635), custom_call_target="InvertDiagBlocksLowerTriangular" | custom-call | tf_op jit(solution)/shard_map/while/body/eval_jaxpr/while/body/eval_jaxpr/triangular_solve/custom-call.6 | solution.py:56
  252.6 13.4 collective-permute-done
  280.6 46.9 %custom-call.71 = f32[4,128,128]{2,1,0:T(8,128)S(1)} custom-call(f32[4,128,128]{2,1,0:T(8,128)S(1)} %cholesky.566), custom_call_target="Cholesky" | custom-call | tf_op jit(solution)/shard_map/while/body/eval_jaxpr/while/body/eval_jaxpr/jit(cholesky)/cholesky | solution.py:50
  328.9 40.8 %custom-call.72 = f32[4,1,128,128]{2,3,1,0:T(8,128)} custom-call(f32[4,1,128,128]{3,2,1,0:T(8,128)} %select_bitcast_fusion.6), custom_call_target="InvertDiagBlocksLowerTriangular" | custom-call | tf_op jit(solution)/shard_map/while/body/eval_jaxpr/while/body/eval_jaxpr/jit(cholesky)/cholesky | solution.py:50
  372.4 47.7 %custom-call.73 = f32[4,128,128]{2,1,0:T(8,128)S(1)} custom-call(f32[4,128,128]{2,1,0:T(8,128)} %convolution_subtract_fusion.33), custom_call_target="Cholesky" | custom-call | tf_op jit(solution)/shard_map/while/body/eval_jaxpr/while/body/eval_jaxpr/jit(cholesky)/cholesky | solution.py:50
  421.7 5.6 while.57
  422.3 2.1 bitcast_dynamic-update-slice_fusion.8
  425.1 2.1 bitcast_dynamic-update-slice_fusion.8
  427.3 79.4 %custom-call.75 = f32[4,2,128,128]{2,3,1,0:T(8,128)S(1)} custom-call(f32[4,2,128,128]{3,2,1,0:T(8,128)} %bitcast.635), custom_call_target="InvertDiagBlocksLowerTriangular" | custom-call | tf_op jit(solution)/shard_map/while/body/eval_jaxpr/while/body/eval_jaxpr/triangular_solve/custom-call.6 | solution.py:56
  511.1 12.6 collective-permute-done
  538.2 46.9 %custom-call.71 = f32[4,128,128]{2,1,0:T(8,128)S(1)} custom-call(f32[4,128,128]{2,1,0:T(8,128)S(1)} %cholesky.566), custom_call_target="Cholesky" | custom-call | tf_op jit(solution)/shard_map/while/body/eval_jaxpr/while/body/eval_jaxpr/jit(cholesky)/cholesky | solution.py:50
  586.5 40.8 %custom-call.72 = f32[4,1,128,128]{2,3,1,0:T(8,128)} custom-call(f32[4,1,128,128]{3,2,1,0:T(8,128)} %select_bitcast_fusion.6), custom_call_target="InvertDiagBlocksLowerTriangular" | custom-call | tf_op jit(solution)/shard_map/while/body/eval_jaxpr/while/body/eval_jaxpr/jit(cholesky)/cholesky | solution.py:50
  630.0 47.7 %custom-call.73 = f32[4,128,128]{2,1,0:T(8,128)S(1)} custom-call(f32[4,128,128]{2,1,0:T(8,128)} %convolution_subtract_fusion.33), custom_call_target="Cholesky" | custom-call | tf_op jit(solution)/shard_map/while/body/eval_jaxpr/while/body/eval_jaxpr/jit(cholesky)/cholesky | solution.py:50
  679.3 5.6 while.57
  679.9 2.1 bitcast_dynamic-update-slice_fusion.8
  682.8 2.1 bitcast_dynamic-update-slice_fusion.8
  684.9 79.4 %custom-call.75 = f32[4,2,128,128]{2,3,1,0:T(8,128)S(1)} custom-call(f32[4,2,128,128]{3,2,1,0:T(8,128)} %bitcast.635), custom_call_target="InvertDiagBlocksLowerTriangular" | custom-call | tf_op jit(solution)/shard_map/while/body/eval_jaxpr/while/body/eval_jaxpr/triangular_solve/custom-call.6 | solution.py:56
  768.7 11.7 collective-permute-done
  788.0 769.9 %while.52 = (s32[]{:T(128)}, f32[4,2,128,128]{2,3,0,1:T(8,128)S(1)}, f32[1,4,2,128,128]{3,4,1,2,0:T(8,128)S(1)}, f32[]{:T(128)}, f32[2,128,128]{1,2,0:T(8,128)S(...) while((s32[]{:T(128)}, ...), condition=%wide.region_5.9_spmd, body=%wide.region_0.8_spmd.sunk | while | flops 2017854464 | bytes 37103660 | solution.py:111
  804.4 46.9 %custom-call.66 = f32[4,128,128]{2,1,0:T(8,128)S(1)} custom-call(f32[4,128,128]{2,1,0:T(8,128)S(1)} %cholesky.540), custom_call_target="Cholesky" | custom-call | tf_op jit(solution)/shard_map/while/body/eval_jaxpr/while/body/eval_jaxpr/jit(cholesky)/cholesky | solution.py:50
  852.7 40.7 %custom-call.67 = f32[4,1,128,128]{2,3,1,0:T(8,128)} custom-call(f32[4,1,128,128]{3,2,1,0:T(8,128)} %select_bitcast_fusion.5), custom_call_target="InvertDiagBlocksLowerTriangular" | custom-call | tf_op jit(solution)/shard_map/while/body/eval_jaxpr/while/body/eval_jaxpr/jit(cholesky)/cholesky | solution.py:50
  896.2 47.7 %custom-call.68 = f32[4,128,128]{2,1,0:T(8,128)S(1)} custom-call(f32[4,128,128]{2,1,0:T(8,128)} %convolution_subtract_fusion.27), custom_call_target="Cholesky" | custom-call | tf_op jit(solution)/shard_map/while/body/eval_jaxpr/while/body/eval_jaxpr/jit(cholesky)/cholesky | solution.py:50
  945.5 5.3 while.56
  946.1 2.0 bitcast_dynamic-update-slice_fusion.9
  948.8 2.0 bitcast_dynamic-update-slice_fusion.9
  950.8 79.4 %custom-call.70 = f32[4,2,128,128]{2,3,1,0:T(8,128)S(1)} custom-call(f32[4,2,128,128]{3,2,1,0:T(8,128)} %bitcast.636), custom_call_target="InvertDiagBlocksLowerTriangular" | custom-call | tf_op jit(solution)/shard_map/while/body/eval_jaxpr/while/body/eval_jaxpr/triangular_solve/custom-call.6 | solution.py:56
  1038.9 2.9 collective-permute-start.1
  1041.8 8.0 collective-permute-done.1
  1058.4 46.9 %custom-call.66 = f32[4,128,128]{2,1,0:T(8,128)S(1)} custom-call(f32[4,128,128]{2,1,0:T(8,128)S(1)} %cholesky.540), custom_call_target="Cholesky" | custom-call | tf_op jit(solution)/shard_map/while/body/eval_jaxpr/while/body/eval_jaxpr/jit(cholesky)/cholesky | solution.py:50
  1106.8 40.7 %custom-call.67 = f32[4,1,128,128]{2,3,1,0:T(8,128)} custom-call(f32[4,1,128,128]{3,2,1,0:T(8,128)} %select_bitcast_fusion.5), custom_call_target="InvertDiagBlocksLowerTriangular" | custom-call | tf_op jit(solution)/shard_map/while/body/eval_jaxpr/while/body/eval_jaxpr/jit(cholesky)/cholesky | solution.py:50
  1150.2 47.7 %custom-call.68 = f32[4,128,128]{2,1,0:T(8,128)S(1)} custom-call(f32[4,128,128]{2,1,0:T(8,128)} %convolution_subtract_fusion.27), custom_call_target="Cholesky" | custom-call | tf_op jit(solution)/shard_map/while/body/eval_jaxpr/while/body/eval_jaxpr/jit(cholesky)/cholesky | solution.py:50
  1199.5 5.3 while.56
  1200.2 2.0 bitcast_dynamic-update-slice_fusion.9
  1202.8 2.0 bitcast_dynamic-update-slice_fusion.9
  1204.8 79.4 %custom-call.70 = f32[4,2,128,128]{2,3,1,0:T(8,128)S(1)} custom-call(f32[4,2,128,128]{3,2,1,0:T(8,128)} %bitcast.636), custom_call_target="InvertDiagBlocksLowerTriangular" | custom-call | tf_op jit(solution)/shard_map/while/body/eval_jaxpr/while/body/eval_jaxpr/triangular_solve/custom-call.6 | solution.py:56
  1292.9 4.1 collective-permute-start.1
  1297.0 7.1 collective-permute-done.1
  1312.8 46.9 %custom-call.66 = f32[4,128,128]{2,1,0:T(8,128)S(1)} custom-call(f32[4,128,128]{2,1,0:T(8,128)S(1)} %cholesky.540), custom_call_target="Cholesky" | custom-call | tf_op jit(solution)/shard_map/while/body/eval_jaxpr/while/body/eval_jaxpr/jit(cholesky)/cholesky | solution.py:50
  1361.2 40.7 %custom-call.67 = f32[4,1,128,128]{2,3,1,0:T(8,128)} custom-call(f32[4,1,128,128]{3,2,1,0:T(8,128)} %select_bitcast_fusion.5), custom_call_target="InvertDiagBlocksLowerTriangular" | custom-call | tf_op jit(solution)/shard_map/while/body/eval_jaxpr/while/body/eval_jaxpr/jit(cholesky)/cholesky | solution.py:50
  1404.6 47.7 %custom-call.68 = f32[4,128,128]{2,1,0:T(8,128)S(1)} custom-call(f32[4,128,128]{2,1,0:T(8,128)} %convolution_subtract_fusion.27), custom_call_target="Cholesky" | custom-call | tf_op jit(solution)/shard_map/while/body/eval_jaxpr/while/body/eval_jaxpr/jit(cholesky)/cholesky | solution.py:50
  1453.9 5.3 while.56
  1454.6 2.0 bitcast_dynamic-update-slice_fusion.9
  1459.2 79.4 %custom-call.70 = f32[4,2,128,128]{2,3,1,0:T(8,128)S(1)} custom-call(f32[4,2,128,128]{3,2,1,0:T(8,128)} %bitcast.636), custom_call_target="InvertDiagBlocksLowerTriangular" | custom-call | tf_op jit(solution)/shard_map/while/body/eval_jaxpr/while/body/eval_jaxpr/triangular_solve/custom-call.6 | solution.py:56
  1547.3 4.1 collective-permute-start.1
  1551.4 6.1 collective-permute-done.1
  1562.8 46.9 %custom-call.34 = f32[1,4,128,128]{3,2,1,0:T(8,128)S(1)} custom-call(f32[1,4,128,128]{3,2,1,0:T(8,128)S(1)} %cholesky.346), custom_call_target="Cholesky" | custom-call | tf_op jit(solution)/shard_map/jit(cholesky)/cholesky | solution.py:50
  1609.8 39.3 %custom-call.35 = f32[1,4,1,128,128]{3,4,2,1,0:T(8,128)S(1)} custom-call(f32[1,4,1,128,128]{4,3,2,1,0:T(8,128)S(1)} %select_bitcast_fusion.2), custom_call_target="InvertDiagBlocksLowerTriangular" | custom-call | tf_op jit(solution)/shard_map/jit(cholesky)/cholesky | solution.py:50
  1650.2 47.1 %custom-call.36 = f32[1,4,128,128]{3,2,1,0:T(8,128)S(1)} custom-call(f32[1,4,128,128]{3,2,1,0:T(8,128)S(1)} %fusion.89), custom_call_target="Cholesky" | custom-call | tf_op jit(solution)/shard_map/jit(cholesky)/cholesky | solution.py:50
  1697.8 5.3 while.55
  1698.4 2.0 bitcast_dynamic-update-slice_fusion.7
  1701.0 2.0 bitcast_dynamic-update-slice_fusion.7
  1703.0 79.4 %custom-call.37 = f32[1,4,2,128,128]{3,4,2,1,0:T(8,128)S(1)} custom-call(f32[1,4,2,128,128]{4,3,2,1,0:T(8,128)} %bitcast.637), custom_call_target="InvertDiagBlocksLowerTriangular" | custom-call | tf_op jit(solution)/shard_map/triangular_solve | solution.py:56
  1785.6 9.4 collective-permute-start.2
  1795.1 4.0 collective-permute-start.4
  1799.1 3.4 collective-permute-start.5
  1802.5 2.1 collective-permute-start.3
  1809.7 5.1 collective-permute-done.4
  (423 shorter events, 188.1 us)
Async XLA Ops:
  2.0 4.8 copy-start.7
  2.0 1.0 copy-start.13
  3.1 0.9 copy-start
  3.2 3.6 copy-start.12
  4.7 0.7 copy-start.14
  6.1 0.8 copy-start.8
  6.8 0.7 copy-start.9
  18.0 1.4 copy-start.1
  69.0 0.7 copy-start.10
  161.6 0.8 copy-start.3
  162.5 0.7 copy-start.19
  251.3 14.7 collective-permute-start
  276.5 1.4 copy-start.1
  327.5 0.7 copy-start.10
  420.1 0.8 copy-start.3
  420.9 0.7 copy-start.19
  509.8 13.9 collective-permute-start
  534.1 1.4 copy-start.1
  585.1 0.7 copy-start.10
  677.7 0.8 copy-start.3
  678.5 0.7 copy-start.19
  767.4 13.1 collective-permute-start
  795.7 0.6 copy-start.5
  800.2 1.4 copy-start.2
  851.3 0.7 copy-start.11
  943.9 0.8 copy-start.4
  944.7 0.7 copy-start.20
  1038.8 10.9 copy-start.6
  1038.9 10.9 collective-permute-start.1
  1049.7 0.6 copy-start.5
  1054.3 1.4 copy-start.2
  1105.3 0.7 copy-start.11
  1197.9 0.8 copy-start.4
  1198.8 0.7 copy-start.20
  1292.8 11.3 copy-start.6
  1292.9 11.2 collective-permute-start.1
  1304.1 0.6 copy-start.5
  1308.7 1.4 copy-start.2
  1359.7 0.7 copy-start.11
  1452.3 0.8 copy-start.4
  1453.2 0.7 copy-start.20
  1547.2 10.3 copy-start.6
  1547.3 10.2 collective-permute-start.1
  1785.6 31.8 %collective-permute-start.2 = (f32[1,4,2,128,128]{4,3,1,2,0:T(8,128)S(1)}, f32[1,4,2,128,128]{4,3,1,2,0:T(8,128)S(1)}, u32[]{:S(2)}, u32[]{:S(2)}) collective-permute-start(f32[1,4,2,128,128]{4,3,1,2,0:T(8,128)S(1)} %get-tuple-element.341), channel_id=1, source_target_pairs={{0,1},{1,2},{2,3},{3,4},{4,5},{5,6},{6,7},{7,8},{8,9},{9,10},{10,1... | collective-permute-start | bytes 1572872 | tf_op jit(solution)/shard_map/ppermute | solution.py:20
  1795.1 19.7 %collective-permute-start.4 = (f32[1,4,2,128,128]{4,3,1,2,0:T(8,128)S(1)}, f32[1,4,2,128,128]{4,3,1,2,0:T(8,128)S(1)}, u32[]{:S(2)}, u32[]{:S(2)}) collective-permute-start(f32[1,4,2,128,128]{4,3,1,2,0:T(8,128)S(1)} %get-tuple-element.341), channel_id=1, source_target_pairs={{0,2},{1,3},{2,4},{3,5},{4,6},{5,7},{6,8},{7,9},{8,10},{9,11},{10,... | collective-permute-start | bytes 1572872 | tf_op jit(solution)/shard_map/ppermute | solution.py:20
  1799.1 17.0 collective-permute-start.5
  1802.5 16.9 collective-permute-start.3
  1804.7 0.7 copy-start.18
  1805.3 0.7 copy-start.15
  1806.1 0.6 copy-start.16
  1806.7 0.7 copy-start.17
where the time goes:
time: 1830 us; the launch traced here: 1820 us
  other arithmetic  1540 us (84%)
  matrix products  106 us (6%)
  local copies, waits for them, and re-layouts  65 us (4%)
  waiting for transfers between devices  64.6 us (4%)
  starting transfers between devices  34 us (2%)
    another operation x63, other arithmetic, invert(): factor_low = jnp.linalg.cholesky(embedded)  955 us
    another operation x34, other arithmetic, invert(): lax.linalg.triangular_solve(factor_low, halfway, left_side=True, lower=Tr...  565 us
    ppermute x10, waiting for transfers between devices, from_behind(): return lax.ppermute(block, axis, route)  64.6 us
  transfers between devices with their start and end apart: 10, of which 8 were waited for; matrix products, arithmetic and copies ran while one was open for 0% of the time, Pallas kernels for 0%

commit v1 on v0

v1 whole, which is shorter than its diff:
```python
import jax
import jax.numpy as jnp
from jax import lax
from jax.experimental import pallas as pl
from jax.experimental.pallas import tpu as pltpu
from jax.sharding import PartitionSpec as P

OFFSET_MAX = 8

PRECISE = lax.Precision.HIGHEST
BROADENING = 0.2
CONTACT_RATE = 0.5
LEAD_WIDTH = 1.0
BAND_LOW = -2.5
BAND_SPAN = 5.0
HALF = 64


def from_behind(block, axis, distance):
    devices = range(lax.axis_size(axis))
    route = [(i - distance, i) for i in devices if i - distance in devices]
    return lax.ppermute(block, axis, route)


def dot(x, y):
    return lax.dot_general(x, y, (((1,), (0,)), ((), ())), precision=PRECISE, preferred_element_type=jnp.float32)

def packed_sign(shape):
    li = lax.broadcasted_iota(jnp.int32, shape, 1)
    return jnp.where(li < HALF, -1.0, 1.0)

def rot(x):
    return pltpu.roll(x, HALF, 1) * packed_sign((1, 2 * HALF))

def pprod(x, y):
    return dot(x, jnp.concatenate([y, rot(y)], axis=0))

def leaves(blocks):
    n = HALF // 8
    li = lax.broadcasted_iota(jnp.int32, (8, 2 * HALF), 1)
    si = lax.broadcasted_iota(jnp.int32, (8, 2 * HALF), 0)
    sign = jnp.where(li < HALF, -1.0, 1.0)
    wide = lambda x: jnp.broadcast_to(x, (8, 2 * HALF))
    tiles = [[b[8 * t:8 * t + 8] for t in range(n)] for b in blocks]
    for g in range(n):
        base = 8 * g
        for rows in tiles:
            panel = rows[g]
            spun = pltpu.roll(panel, HALF, 1) * sign
            cr = [wide(panel[:, base + j:base + j + 1]) for j in range(8)]
            ci = [wide(panel[:, HALF + base + j:HALF + base + j + 1]) for j in range(8)]
            for k in range(8):
                pr, pi = wide(cr[k][k:k + 1]), wide(ci[k][k:k + 1])
                d = 1.0 / (pr * pr + pi * pi)
                ir, ii = pr * d, -pi * d
                row = wide(panel[k:k + 1]) + jnp.where(li == base + k, 1.0, 0.0)
                turn = wide(spun[k:k + 1]) + jnp.where(li == HALF + base + k, 1.0, 0.0)
                v = ir * row + ii * turn
                vt = ir * turn - ii * row
                ur, ui = cr[k] - jnp.where(si == k, 1.0, 0.0), ci[k]
                for j in range(k + 1, 8):
                    xr, xi = wide(cr[j][k:k + 1]), wide(ci[j][k:k + 1])
                    wr = ir * xr - ii * xi
                    wi = ir * xi + ii * xr
                    cr[j] = cr[j] - (ur * wr - ui * wi)
                    ci[j] = ci[j] - (ur * wi + ui * wr)
                panel = panel - (ur * v + ui * vt)
                spun = spun - (ur * vt - ui * v)
            full = panel + jnp.where(li == base + si, 1.0, 0.0)
            turned = spun + jnp.where(li == HALF + base + si, 1.0, 0.0)
            fr = [wide(full[j:j + 1]) for j in range(8)]
            ft = [wide(turned[j:j + 1]) for j in range(8)]
            order = [t for t in range(g + 1, n)] + [t for t in range(g)]
            for t in order:
                x = rows[t]
                terms = [wide(x[:, base + j:base + j + 1]) * fr[j] + wide(x[:, HALF + base + j:HALF + base + j + 1]) * ft[j] for j in range(8)]
                while len(terms) > 1:
                    terms = [p + q for p, q in zip(terms[::2], terms[1::2])]
                rows[t] = x - terms[0]
            rows[g] = panel
    return [jnp.concatenate(rows, axis=0) for rows in tiles]

def quads(x):
    re, im = x
    def q(p, c):
        rows = slice(HALF * p, HALF * (p + 1)); cols = slice(HALF * c, HALF * (c + 1))
        return jnp.concatenate([re[rows, cols], im[rows, cols]], axis=1)
    return q(0, 0), q(0, 1), q(1, 0), q(1, 1)

def planes(qs):
    q00, q01, q10, q11 = qs
    re = jnp.concatenate([jnp.concatenate([q00[:, :HALF], q01[:, :HALF]], 1), jnp.concatenate([q10[:, :HALF], q11[:, :HALF]], 1)], 0)
    im = jnp.concatenate([jnp.concatenate([q00[:, HALF:], q01[:, HALF:]], 1), jnp.concatenate([q10[:, HALF:], q11[:, HALF:]], 1)], 0)
    return re, im

def invert_all(mats):
    qs = [quads(m) for m in mats]
    firsts = leaves([q[0] for q in qs])
    ts, ss, us = [], [], []
    for q, f in zip(qs, firsts):
        t = pprod(q[2], f)
        ts.append(t); us.append(pprod(f, q[1]))
        ss.append(q[3] - pprod(t, q[1]))
    seconds = leaves(ss)
    outs = []
    for f, t, u, s in zip(firsts, ts, us, seconds):
        lower = pprod(s, t)
        outs.append(planes((f + pprod(u, lower), -pprod(u, s), -lower, s)))
    return outs

def cprod(x, y):
    xr, xi = x; yr, yi = y
    lhs = jnp.concatenate([xr, xi], axis=1)
    rhs = jnp.concatenate([jnp.concatenate([yr, yi], 1), jnp.concatenate([-yi, yr], 1)], 0)
    out = dot(lhs, rhs)
    n = yr.shape[1]
    return out[:, :n], out[:, n:]

def adj(x):
    return x[0].T, -x[1].T

def add(x, y): return x[0] + y[0], x[1] + y[1]
def sub(x, y): return x[0] - y[0], x[1] - y[1]

def solve(a, v):
    v0, v1, v2 = v
    h0, h1, h2 = adj(v0), adj(v1), adj(v2)
    g0, g3 = invert_all([a[0], a[3]])
    t0 = cprod(g0, v0)
    d1 = sub(a[1], cprod(h0, t0))
    u3 = cprod(g3, h2)
    d2 = sub(a[2], cprod(v2, u3))
    g2, = invert_all([d2])
    w = cprod(g2, h1)
    green1, = invert_all([sub(d1, cprod(v1, w))])
    green2 = add(g2, cprod(w, cprod(green1, cprod(v1, g2))))
    green0 = add(g0, cprod(t0, cprod(green1, cprod(h0, g0))))
    green3 = add(g3, cprod(u3, cprod(green2, cprod(v2, g3))))
    return green0, green1, green2, green3

def comp_kernel(a_ref, v_ref, g_ref):
    a = [(a_ref[c, 0], a_ref[c, 1]) for c in range(4)]
    v = [(v_ref[c, 0], v_ref[c, 1]) for c in range(3)]
    for c, g in enumerate(solve(a, v)):
        g_ref[c, 0] = g[0]
        g_ref[c, 1] = g[1]

def per_device(hamiltonian, coupling, sigma_in, mode_offsets, mode_coupling, energy_owner):
    slot_count = sigma_in.shape[1]
    orbitals = hamiltonian.shape[-1]
    chain_length = lax.axis_size("cell")
    energy_devices = lax.axis_size("energy")
    chain_index = lax.axis_index("cell")
    energy_index = lax.axis_index("energy")
    energy_count = slot_count * energy_devices
    identity = jnp.eye(orbitals, dtype=jnp.float32)
    at_start = (chain_index == 0).astype(jnp.float32)
    at_end = (chain_index == chain_length - 1).astype(jnp.float32)
    my_owner = lax.dynamic_slice_in_dim(energy_owner, energy_index * slot_count, slot_count)
    energy_level = BAND_LOW + BAND_SPAN * my_owner.astype(jnp.float32) / (energy_count - 1)
    last_r, last_i = coupling[0, 0], coupling[0, 1]
    mm = lambda x, y: jnp.matmul(x, y.T, precision=PRECISE)
    beyond_r = mm(last_r, last_r) + mm(last_i, last_i)
    beyond_i = mm(last_i, last_r) - mm(last_r, last_i)
    fold_r = -LEAD_WIDTH * at_end * beyond_i
    fold_i = LEAD_WIDTH * at_end * beyond_r + (BROADENING + CONTACT_RATE * at_start) * identity
    fold = jnp.stack([fold_r, fold_i])
    level = energy_level[:, None, None, None] * jnp.stack([identity, jnp.zeros_like(identity)])[None]
    block = level + fold[None] - hamiltonian - sigma_in[0]
    mine = lax.all_to_all(block, "cell", 0, 0)
    links = lax.all_gather(coupling[0], "cell")
    green = pl.pallas_call(
        comp_kernel, out_shape=jax.ShapeDtypeStruct(mine.shape, jnp.float32)
    )(mine, links)
    green_diag = lax.all_to_all(green, "cell", 0, 0)[None]

    def weight_rows(source_owner):
        offset_table = source_owner[None, :] - my_owner[:, None]
        matches = (offset_table[:, :, None] == -mode_offsets).astype(jnp.float32) + (
            offset_table[:, :, None] == mode_offsets
        ).astype(jnp.float32)
        return jnp.sum(matches * mode_coupling, -1)

    def contribute(running_sum, blocks, device_offset):
        first_slot = jnp.clip(
            (energy_index - device_offset) * slot_count, 0, energy_count - slot_count
        )
        source_owner = lax.dynamic_slice_in_dim(energy_owner, first_slot, slot_count)
        weights = weight_rows(source_owner)
        return running_sum + jnp.einsum("sk,ckrij->csrij", weights, blocks, precision=PRECISE)

    reach = min(-(-OFFSET_MAX // slot_count), energy_devices - 1)
    sigma_out = contribute(jnp.zeros_like(green_diag), green_diag, 0)
    for distance in range(1, reach + 1):
        for direction in (1, -1):
            arrived = from_behind(green_diag, "energy", direction * distance)
            sigma_out = contribute(sigma_out, arrived, direction * distance)
    return (green_diag, sigma_out)


def solution(mesh):
    in_specs = (
        P("cell", None, None, None),
        P("cell", None, None, None),
        P("cell", "energy", None, None, None),
        P(),
        P(),
        P(),
    )
    out_specs = (P("cell", "energy", None, None, None), P("cell", "energy", None, None, None))
    return jax.shard_map(
        per_device, mesh=mesh, in_specs=in_specs, out_specs=out_specs, check_vma=False
    )
```

time: 1830 us -> 97.9 us (0.05)
  the two profiles are of different devices: /device:TPU:25 before, /device:TPU:105 now
where the time goes in v1:
time: 97.9 us; the launch traced here: 97.5 us
  Pallas kernels  30.8 us (31%)
  starting transfers between devices  25.1 us (26%)
  blocking collectives  14.8 us (15%)
  waiting for transfers between devices  11.3 us (12%)
  matrix products  8.68 us (9%)
  local copies, waits for them, and re-layouts  4.71 us (5%)
  other arithmetic  1.32 us (1%)
    pallas_call x1, Pallas kernels, per_device(): pl.pallas_call(comp_kernel, out_shape=jax.ShapeDtypeStruct(mine.shape, jn...  30.8 us
    ppermute x4, starting transfers between devices, from_behind(): return lax.ppermute(block, axis, route)  17.6 us
    all_gather x1, blocking collectives, per_device(): links = lax.all_gather(coupling[0], 'cell')  14.8 us
    dot_general x5, matrix products, contribute(): jnp.einsum('sk,ckrij->csrij', weights, blocks, precision=PRECISE)  6.65 us
    all_to_all x1, waiting for transfers between devices, per_device(): green_diag = lax.all_to_all(green, 'cell', 0, 0)[None]  6.13 us
    ppermute x4, waiting for transfers between devices, from_behind(): return lax.ppermute(block, axis, route)  5.16 us
    unnamed x16, local copies, waits for them, and re-layouts  4.63 us
    all_to_all x1, starting transfers between devices, per_device(): mine = lax.all_to_all(block, 'cell', 0, 0)  4.01 us
  transfers between devices with their start and end apart: 6, of which 2 were waited for; matrix products, arithmetic and copies ran while one was open for 6% of the time, Pallas kernels for 0%

profile of v1, /device:TPU:105, one launch (start us, length us, event | category | flops | bytes accessed | tf_op | source)
XLA Modules:
  0.0 97.5 jit_solution(10758219014807217049)
XLA Ops:
  0.6 0.0 copy-start.1
  0.6 0.0 copy-start.4
  0.7 1.2 %fusion.16 = f32[128,128]{1,0:T(8,128)S(1)} fusion(f32[1,2,128,128]{3,2,1,0:T(8,128)} %param.7), kind=kOutput, calls=%fused_computation.23 | convolution fusion | flops 25165824 | bytes 131072 | tf_op jit(solution)/shard_map/dot_general | solution.py:162
  1.9 0.0 copy-done.1
  1.9 0.0 copy-start.2
  1.9 0.3 fusion.19
  2.2 0.0 copy-done.4
  2.2 0.1 multiply_add_fusion
  2.3 0.3 fusion.7
  2.6 0.3 fusion.5
  2.9 0.0 copy-start.3
  2.9 0.0 copy-done.2
  2.9 0.8 copy-done.3
  3.8 0.9 bitcast_subtract_fusion
  4.7 4.0 %all-to-all-start = ((f32[4,2,128,128]{3,2,1,0:T(8,128)}), f32[4,2,128,128]{3,2,1,0:T(8,128)S(1)}, u32[]{:S(2)}, u32[]{:S(2)}) async-start(f32[4,2,128,128]{3,2,1,0:T(8,128)} %bitcast_subtract_fusion), calls=%async_computation | async-start | bytes 1048576 | tf_op jit(solution)/shard_map/all_to_all | solution.py:170
  8.7 14.8 %all_gather.3.v_ref = f32[4,2,128,128]{3,2,1,0:T(8,128)} all-gather(f32[1,2,128,128]{3,2,1,0:T(8,128)S(1)} %copy-done.1), channel_id=1, replica_groups=mesh['cell'=4,'energy'=32] {'cell'}, dimensions={0}, use_global_device_ids=true | all-gather | bytes 655360 | tf_op jit(solution)/shard_map/all_gather | solution.py:171
  23.5 0.0 all-to-all-done.a_ref
  23.5 0.0 copy-start
  23.5 0.8 copy-done
  24.3 30.8 %shard_map.77 = f32[4,2,128,128]{3,2,1,0:T(8,128)} custom-call(f32[4,2,128,128]{3,2,1,0:T(8,128)} %copy-done, f32[4,2,128,128]{3,2,1,0:T(8,128)} %all_gather.3.v_ref), custom_call_target="tpu_custom_call" | custom-call | tf_op jit(solution)/shard_map/pallas_call | solution.py:172
  55.1 3.5 %all-to-all-start.1 = ((f32[4,2,128,128]{3,2,1,0:T(8,128)}), f32[4,2,128,128]{3,2,1,0:T(8,128)S(1)}, u32[]{:S(2)}, u32[]{:S(2)}) async-start(f32[4,2,128,128]{3,2,1,0:T(8,128)} %shard_map.77), calls=%async_computation.1 | async-start | bytes 1048576 | tf_op jit(solution)/shard_map/all_to_all | solution.py:175
  58.6 0.0 copy-start.6
  58.6 0.6 copy-done.6
  59.2 0.1 fusion.35
  59.3 6.1 %all-to-all-done.1 = f32[4,2,128,128]{3,2,1,0:T(8,128)S(1)} async-done(((f32[4,2,128,128]{3,2,1,0:T(8,128)}), f32[4,2,128,128]{3,2,1,0:T(8,128)S(1)}, u32[]{:S(2)}, u32[]{:S(2)}) %all-to-all-start.1) | async-done | bytes 524320 | tf_op jit(solution)/shard_map/all_to_all | solution.py:175
  65.5 1.9 %collective-permute-start.2 = (f32[1,4,2,128,128]{4,3,2,1,0:T(8,128)S(1)}, f32[1,4,2,128,128]{4,3,2,1,0:T(8,128)S(1)}, u32[]{:S(2)}, u32[]{:S(2)}) collective-permute-start(f32[1,4,2,128,128]{4,3,2,1,0:T(8,128)S(1)} %bitcast.55), channel_id=1, source_target_pairs={{0,2},{1,3},{2,4},{3,5},{4,6},{5,7},{6,8},{7,9},{8,10},{9,11},{10,... | collective-permute-start | bytes 1572872 | tf_op jit(solution)/shard_map/ppermute | solution.py:22
  67.4 0.1 broadcast_subtract_fusion.4
  67.4 3.4 %collective-permute-start.3 = (f32[1,4,2,128,128]{4,3,2,1,0:T(8,128)S(1)}, f32[1,4,2,128,128]{4,3,2,1,0:T(8,128)S(1)}, u32[]{:S(2)}, u32[]{:S(2)}) collective-permute-start(f32[1,4,2,128,128]{4,3,2,1,0:T(8,128)S(1)} %bitcast.56), channel_id=1, source_target_pairs={{2,0},{3,1},{4,2},{5,3},{6,4},{7,5},{8,6},{9,7},{10,8},{11,9},{12,... | collective-permute-start | bytes 1572872 | tf_op jit(solution)/shard_map/ppermute | solution.py:22
  70.8 0.0 copy-start.5
  70.8 0.6 copy-done.5
  71.5 0.2 multiply_reduce_fusion.2
  71.7 10.2 %collective-permute-start = (f32[1,4,2,128,128]{4,3,2,1,0:T(8,128)S(1)}, f32[1,4,2,128,128]{4,3,2,1,0:T(8,128)S(1)}, u32[]{:S(2)}, u32[]{:S(2)}) collective-permute-start(f32[1,4,2,128,128]{4,3,2,1,0:T(8,128)S(1)} %bitcast.57), channel_id=1, source_target_pairs={{0,1},{1,2},{2,3},{3,4},{4,5},{5,6},{6,7},{7,8},{8,9},{9,10},{10,1... | collective-permute-start | bytes 1572872 | tf_op jit(solution)/shard_map/ppermute | solution.py:22
  81.9 2.1 %collective-permute-start.1 = (f32[1,4,2,128,128]{4,3,2,1,0:T(8,128)S(1)}, f32[1,4,2,128,128]{4,3,2,1,0:T(8,128)S(1)}, u32[]{:S(2)}, u32[]{:S(2)}) collective-permute-start(f32[1,4,2,128,128]{4,3,2,1,0:T(8,128)S(1)} %bitcast.58), channel_id=1, source_target_pairs={{1,0},{2,1},{3,2},{4,3},{5,4},{6,5},{7,6},{8,7},{9,8},{10,9},{11,1... | collective-permute-start | bytes 1572872 | tf_op jit(solution)/shard_map/ppermute | solution.py:22
  84.0 1.3 %fusion.14 = f32[2,128,128,4]{2,3,1,0:T(4,128)S(1)} fusion(f32[4,2,128,128]{3,2,1,0:T(8,128)S(1)} %all-to-all-done.1, f32[4,4]{1,0:T(4,128)S(1)} %get-tuple-element.12), kind=kOutput, calls=%fused_computation.19 | convolution fusion | flops 6291456 | bytes 1048640 | tf_op jit(solution)/shard_map/sk,ckrij->csrij/dot_general | solution.py:190
  85.3 0.0 collective-permute-done.2
  85.4 1.3 %fusion.10 = f32[2,128,128,4]{2,3,1,0:T(4,128)S(1)} fusion(f32[4,2,128,128]{3,2,1,0:T(8,128)S(1)} %bitcast.60, f32[4,4]{1,0:T(4,128)S(1)} %get-tuple-element.10), kind=kOutput, calls=%fused_computation.15 | convolution fusion | flops 6291456 | bytes 1048640 | tf_op jit(solution)/shard_map/sk,ckrij->csrij/dot_general | solution.py:190
  86.7 0.0 collective-permute-done.3
  86.7 1.3 %fusion.8 = f32[2,128,128,4]{2,3,1,0:T(4,128)S(1)} fusion(f32[4,2,128,128]{3,2,1,0:T(8,128)S(1)} %bitcast.61, f32[4,4]{1,0:T(4,128)S(1)} %get-tuple-element.11), kind=kOutput, calls=%fused_computation.13 | convolution fusion | flops 6291456 | bytes 1048640 | tf_op jit(solution)/shard_map/sk,ckrij->csrij/dot_general | solution.py:190
  88.0 0.0 collective-permute-done
  88.0 1.3 %convolution_add_fusion.1 = f32[2,128,128,4]{2,3,1,0:T(4,128)S(1)} fusion(f32[2,128,128,4]{2,3,1,0:T(4,128)S(1)} %fusion.14, f32[4,2,128,128]{3,2,1,0:T(8,128)S(1)} %bitcast.62, f32[4,4]{1,0:T(4,128)S(1)} %get-tuple-element.9), kind=kOutput, calls=%fused_computation.1 | convolution fusion | flops 6422528 | bytes 1572928 | tf_op jit(solution)/shard_map/sk,ckrij->csrij/dot_general | solution.py:190
  89.3 5.2 %collective-permute-done.1 = f32[1,4,2,128,128]{4,3,2,1,0:T(8,128)S(1)} collective-permute-done((f32[1,4,2,128,128]{4,3,2,1,0:T(8,128)S(1)}, f32[1,4,2,128,128]{4,3,2,1,0:T(8,128)S(1)}, u32[]{:S(2)}, u32[]{:S(2)}) %collective-permute-start.1) | collective-permute-done | bytes 524320 | tf_op jit(solution)/shard_map/ppermute | solution.py:22
  94.5 1.4 %fusion.2 = f32[1,4,2,128,128]{4,1,3,2,0:T(4,128)S(1)} fusion(f32[2,128,128,4]{2,3,1,0:T(4,128)S(1)} %fusion.8, f32[2,128,128,4]{2,3,1,0:T(4,128)S(1)} %fusion.10, f32[2,128,128,4]{2,3,1,0:T(4,128)S(1)} %convolution_add_fusion.1, f32[4,2,128,128]{3,2,1,0:T(8,128)S(1)} %bitcast.63, f32[4,4]{1,0:T(4,128)S(1)} %get-tuple-element.8), kind=kOutput, calls=%fused_computation.4 | convolution fusion | flops 6684672 | bytes 2621504 | tf_op jit(solution)/shard_map/sk,ckrij->csrij/dot_general | solution.py:190
  95.9 0.8 copy.25
  96.7 0.8 copy.42
  (4 shorter events, 0.0 us)
Async XLA Ops:
  0.6 1.3 %copy-start.1 = (f32[1,2,128,128]{3,2,1,0:T(8,128)S(1)}, f32[1,2,128,128]{3,2,1,0:T(8,128)}, u32[]{:S(2)}) copy-start(f32[1,2,128,128]{3,2,1,0:T(8,128)} %param.7) | copy-start | bytes 393220
  0.6 1.6 %copy-start.4 = (s32[128]{0:T(128)S(1)}, s32[128]{0:T(128)}, u32[]{:S(2)}) copy-start(s32[128]{0:T(128)} %param.11) | copy-start | bytes 1540
  1.9 1.0 %copy-start.2 = (f32[1,4,2,128,128]{4,3,2,1,0:T(8,128)S(1)}, f32[1,4,2,128,128]{4,3,2,1,0:T(8,128)}, u32[]{:S(2)}) copy-start(f32[1,4,2,128,128]{4,3,2,1,0:T(8,128)} %param.8) | copy-start | bytes 1572868
  2.9 0.9 copy-start.3
  4.7 18.8 %all-to-all-start = ((f32[4,2,128,128]{3,2,1,0:T(8,128)}), f32[4,2,128,128]{3,2,1,0:T(8,128)S(1)}, u32[]{:S(2)}, u32[]{:S(2)}) async-start(f32[4,2,128,128]{3,2,1,0:T(8,128)} %bitcast_subtract_fusion), calls=%async_computation | async-start | bytes 1048576 | tf_op jit(solution)/shard_map/all_to_all | solution.py:170
  23.5 0.8 copy-start
  55.1 10.4 %all-to-all-start.1 = ((f32[4,2,128,128]{3,2,1,0:T(8,128)}), f32[4,2,128,128]{3,2,1,0:T(8,128)S(1)}, u32[]{:S(2)}, u32[]{:S(2)}) async-start(f32[4,2,128,128]{3,2,1,0:T(8,128)} %shard_map.77), calls=%async_computation.1 | async-start | bytes 1048576 | tf_op jit(solution)/shard_map/all_to_all | solution.py:175
  58.6 0.7 copy-start.6
  65.5 19.9 %collective-permute-start.2 = (f32[1,4,2,128,128]{4,3,2,1,0:T(8,128)S(1)}, f32[1,4,2,128,128]{4,3,2,1,0:T(8,128)S(1)}, u32[]{:S(2)}, u32[]{:S(2)}) collective-permute-start(f32[1,4,2,128,128]{4,3,2,1,0:T(8,128)S(1)} %bitcast.55), channel_id=1, source_target_pairs={{0,2},{1,3},{2,4},{3,5},{4,6},{5,7},{6,8},{7,9},{8,10},{9,11},{10,... | collective-permute-start | bytes 1572872 | tf_op jit(solution)/shard_map/ppermute | solution.py:22
  67.4 19.2 %collective-permute-start.3 = (f32[1,4,2,128,128]{4,3,2,1,0:T(8,128)S(1)}, f32[1,4,2,128,128]{4,3,2,1,0:T(8,128)S(1)}, u32[]{:S(2)}, u32[]{:S(2)}) collective-permute-start(f32[1,4,2,128,128]{4,3,2,1,0:T(8,128)S(1)} %bitcast.56), channel_id=1, source_target_pairs={{2,0},{3,1},{4,2},{5,3},{6,4},{7,5},{8,6},{9,7},{10,8},{11,9},{12,... | collective-permute-start | bytes 1572872 | tf_op jit(solution)/shard_map/ppermute | solution.py:22
  70.8 0.7 copy-start.5
  71.7 16.4 %collective-permute-start = (f32[1,4,2,128,128]{4,3,2,1,0:T(8,128)S(1)}, f32[1,4,2,128,128]{4,3,2,1,0:T(8,128)S(1)}, u32[]{:S(2)}, u32[]{:S(2)}) collective-permute-start(f32[1,4,2,128,128]{4,3,2,1,0:T(8,128)S(1)} %bitcast.57), channel_id=1, source_target_pairs={{0,1},{1,2},{2,3},{3,4},{4,5},{5,6},{6,7},{7,8},{8,9},{9,10},{10,1... | collective-permute-start | bytes 1572872 | tf_op jit(solution)/shard_map/ppermute | solution.py:22
  81.9 12.6 %collective-permute-start.1 = (f32[1,4,2,128,128]{4,3,2,1,0:T(8,128)S(1)}, f32[1,4,2,128,128]{4,3,2,1,0:T(8,128)S(1)}, u32[]{:S(2)}, u32[]{:S(2)}) collective-permute-start(f32[1,4,2,128,128]{4,3,2,1,0:T(8,128)S(1)} %bitcast.58), channel_id=1, source_target_pairs={{1,0},{2,1},{3,2},{4,3},{5,4},{6,5},{7,6},{8,7},{9,8},{10,9},{11,1... | collective-permute-start | bytes 1572872 | tf_op jit(solution)/shard_map/ppermute | solution.py:22

commit v2 on v1

--- a/solution.py
+++ b/solution.py
@@ -14,12 +14,6 @@
 BAND_LOW = -2.5
 BAND_SPAN = 5.0
 HALF = 64
-
-
-def from_behind(block, axis, distance):
-    devices = range(lax.axis_size(axis))
-    route = [(i - distance, i) for i in devices if i - distance in devices]
-    return lax.ppermute(block, axis, route)
 
 
 def dot(x, y):
@@ -145,6 +139,251 @@
         g_ref[c, 0] = g[0]
         g_ref[c, 1] = g[1]
 
+MESH = pl.DeviceIdType.MESH
+ARRIVALS = (1, 3, 2)
+
+
+def remote(source, target, sent, landed, where):
+    return pltpu.make_async_remote_copy(
+        src_ref=source, dst_ref=target, send_sem=sent, recv_sem=landed,
+        device_id=where, device_id_type=MESH,
+    )
+
+
+def gather_kernel(block_ref, link_ref, mine_ref, links_ref, a_sent, a_landed, v_sent, v_landed):
+    cells = 4
+    me = lax.axis_index("cell")
+    other = lambda distance: lax.rem(me + distance, cells)
+    barrier = pltpu.get_barrier_semaphore()
+    for distance in ARRIVALS:
+        pl.semaphore_signal(barrier, 1, device_id={"cell": other(distance)}, device_id_type=MESH)
+    pl.semaphore_wait(barrier, cells - 1)
+
+    def a_copy(distance, owner):
+        return remote(block_ref.at[other(distance)], mine_ref.at[owner], a_sent.at[distance - 1],
+                      a_landed.at[owner], {"cell": other(distance)})
+
+    def v_copy(distance, owner):
+        return remote(link_ref.at[0], links_ref.at[owner], v_sent.at[distance - 1],
+                      v_landed.at[owner], {"cell": other(distance)})
+
+    for distance in ARRIVALS:
+        a_copy(distance, me).start()
+
+    @pl.when(me < cells - 1)
+    def _():
+        for distance in ARRIVALS:
+            v_copy(distance, me).start()
+        links_ref[me] = link_ref[0]
+
+    mine_ref[me] = block_ref[me]
+    for distance in ARRIVALS:
+        a_copy(distance, other(cells - distance)).wait_recv()
+
+        @pl.when(other(cells - distance) < cells - 1)
+        def _():
+            v_copy(distance, other(cells - distance)).wait_recv()
+    for distance in ARRIVALS:
+        a_copy(distance, me).wait_send()
+
+    @pl.when(me < cells - 1)
+    def _():
+        for distance in ARRIVALS:
+            v_copy(distance, me).wait_send()
+
+
+def spread_kernel(weights_ref, green_ref, diag_ref, sigma_ref, near, x_sent, x_landed, z_sent, f_sent, landed):
+    cells = 4
+    me = lax.axis_index("cell")
+    energy = lax.axis_index("energy")
+    energies = lax.axis_size("energy")
+    core = lax.rem(energy, 2)
+    partner = energy + 1 - 2 * core
+    lower, upper = energy >= 2, energy < energies - 2
+    other = lambda distance: lax.rem(me + distance, cells)
+    barrier = pltpu.get_barrier_semaphore()
+
+    def greet(where):
+        pl.semaphore_signal(barrier, 1, device_id=where, device_id_type=MESH)
+
+    for distance in ARRIVALS:
+        greet({"cell": other(distance)})
+    greet({"energy": partner})
+
+    @pl.when(lower)
+    def _():
+        greet({"energy": energy - 2})
+
+    @pl.when(upper)
+    def _():
+        greet({"energy": energy + 2})
+    pl.semaphore_wait(barrier, cells + lower.astype(jnp.int32) + upper.astype(jnp.int32))
+
+    def x_copy(distance, slot):
+        return remote(green_ref.at[other(distance)], diag_ref.at[slot], x_sent.at[distance - 1],
+                      x_landed.at[slot], {"cell": other(distance)})
+
+    def from_slot(step):
+        return me if step == 0 else other(cells - ARRIVALS[step - 1])
+
+    def source(step):
+        return green_ref.at[me] if step == 0 else diag_ref.at[from_slot(step)]
+
+    def up(step):
+        slot = from_slot(step)
+        return remote(source(step), near.at[0, slot], z_sent.at[0, step], landed.at[0, slot], {"energy": energy + 2})
+
+    def down(step):
+        slot = from_slot(step)
+        return remote(source(step), near.at[3, slot], z_sent.at[1, step], landed.at[3, slot], {"energy": energy - 2})
+
+    def across(step):
+        slot = from_slot(step)
+        return remote(source(step), near.at[1 + core, slot], z_sent.at[2, step], landed.at[1 + core, slot], {"energy": partner})
+
+    def forward(step, sees, place):
+        slot = from_slot(step)
+        return remote(near.at[sees, slot], near.at[place, slot], f_sent.at[step], landed.at[place, slot], {"energy": partner})
+
+    def arrived(side, step):
+        slot = from_slot(step)
+        remote(near.at[side, slot], near.at[side, slot], f_sent.at[step], landed.at[side, slot], {"energy": partner}).wait_recv()
+
+    for distance in ARRIVALS:
+        x_copy(distance, me).start()
+
+    def send(step):
+        @pl.when(upper)
+        def _():
+            up(step).start()
+
+        @pl.when(lower)
+        def _():
+            down(step).start()
+        across(step).start()
+
+    def receive_x(step):
+        distance = ARRIVALS[step - 1]
+        x_copy(distance, other(cells - distance)).wait_recv()
+        send(step)
+
+    def relay(step):
+        @pl.when(lower)
+        def _():
+            arrived(0, step)
+
+            @pl.when(core == 1)
+            def _():
+                forward(step, 0, 1).start()
+
+        @pl.when(upper)
+        def _():
+            arrived(3, step)
+
+            @pl.when(core == 0)
+            def _():
+                forward(step, 3, 2).start()
+
+    def finish(step):
+        @pl.when(jnp.logical_or(core == 1, lower))
+        def _():
+            arrived(1, step)
+
+        @pl.when(jnp.logical_or(core == 0, upper))
+        def _():
+            arrived(2, step)
+        slot = from_slot(step)
+        blocks = [near[0, slot], near[1, slot], diag_ref[slot], near[2, slot], near[3, slot]]
+        for q in range(4):
+            total = weights_ref[q, slot] * blocks[0]
+            for o in range(1, 5):
+                total += weights_ref[q, 4 * o + slot] * blocks[o]
+            sigma_ref[q] = total if step == 0 else sigma_ref[q] + total
+
+    send(0)
+    diag_ref[me] = green_ref[me]
+    zero = jnp.zeros(near.shape[1:], jnp.float32)
+
+    @pl.when(jnp.logical_not(lower))
+    def _():
+        near[0] = zero
+
+        @pl.when(core == 0)
+        def _():
+            near[1] = zero
+
+    @pl.when(jnp.logical_not(upper))
+    def _():
+        near[3] = zero
+
+        @pl.when(core == 1)
+        def _():
+            near[2] = zero
+    receive_x(1)
+    receive_x(2)
+    relay(0)
+    receive_x(3)
+    relay(1)
+    finish(0)
+    relay(2)
+    finish(1)
+    relay(3)
+    finish(2)
+    finish(3)
+    for distance in ARRIVALS:
+        x_copy(distance, me).wait_send()
+    for step in range(4):
+        @pl.when(upper)
+        def _():
+            up(step).wait_send()
+
+        @pl.when(lower)
+        def _():
+            down(step).wait_send()
+        across(step).wait_send()
+
+        @pl.when(jnp.logical_and(core == 1, lower))
+        def _():
+            forward(step, 0, 1).wait_send()
+
+        @pl.when(jnp.logical_and(core == 0, upper))
+        def _():
+            forward(step, 3, 2).wait_send()
+
+
+def gather(block, links):
+    vmem = pl.BlockSpec(memory_space=pltpu.VMEM)
+    dma = pltpu.SemaphoreType.DMA
+    return pl.pallas_call(
+        gather_kernel,
+        out_shape=(
+            jax.ShapeDtypeStruct(block.shape, jnp.float32),
+            jax.ShapeDtypeStruct((3,) + block.shape[1:], jnp.float32),
+        ),
+        in_specs=[vmem, vmem],
+        out_specs=(vmem, vmem),
+        scratch_shapes=[dma((3,)), dma((4,)), dma((3,)), dma((3,))],
+        compiler_params=pltpu.CompilerParams(collective_id=0, has_side_effects=True),
+    )(block, links)
+
+
+def spread(weights, green):
+    vmem = pl.BlockSpec(memory_space=pltpu.VMEM)
+    dma = pltpu.SemaphoreType.DMA
+    shape = jax.ShapeDtypeStruct(green.shape, jnp.float32)
+    return pl.pallas_call(
+        spread_kernel,
+        out_shape=(shape, shape),
+        in_specs=[pl.BlockSpec(memory_space=pltpu.SMEM), vmem],
+        out_specs=(vmem, vmem),
+        scratch_shapes=[
+            pltpu.VMEM((4,) + green.shape, jnp.float32),
+            dma((3,)), dma((4,)), dma((3, 4)), dma((4,)), dma((4, 4)),
+        ],
+        compiler_params=pltpu.CompilerParams(collective_id=1, has_side_effects=True),
+    )(weights, green)
+
+
 def per_device(hamiltonian, coupling, sigma_in, mode_offsets, mode_coupling, energy_owner):
     slot_count = sigma_in.shape[1]
     orbitals = hamiltonian.shape[-1]
@@ -167,35 +406,16 @@
     fold = jnp.stack([fold_r, fold_i])
     level = energy_level[:, None, None, None] * jnp.stack([identity, jnp.zeros_like(identity)])[None]
     block = level + fold[None] - hamiltonian - sigma_in[0]
-    mine = lax.all_to_all(block, "cell", 0, 0)
-    links = lax.all_gather(coupling[0], "cell")
+    mine, links = gather(block, coupling)
     green = pl.pallas_call(
         comp_kernel, out_shape=jax.ShapeDtypeStruct(mine.shape, jnp.float32)
     )(mine, links)
-    green_diag = lax.all_to_all(green, "cell", 0, 0)[None]
-
-    def weight_rows(source_owner):
-        offset_table = source_owner[None, :] - my_owner[:, None]
-        matches = (offset_table[:, :, None] == -mode_offsets).astype(jnp.float32) + (
-            offset_table[:, :, None] == mode_offsets
-        ).astype(jnp.float32)
-        return jnp.sum(matches * mode_coupling, -1)
-
-    def contribute(running_sum, blocks, device_offset):
-        first_slot = jnp.clip(
-            (energy_index - device_offset) * slot_count, 0, energy_count - slot_count
-        )
-        source_owner = lax.dynamic_slice_in_dim(energy_owner, first_slot, slot_count)
-        weights = weight_rows(source_owner)
-        return running_sum + jnp.einsum("sk,ckrij->csrij", weights, blocks, precision=PRECISE)
-
-    reach = min(-(-OFFSET_MAX // slot_count), energy_devices - 1)
-    sigma_out = contribute(jnp.zeros_like(green_diag), green_diag, 0)
-    for distance in range(1, reach + 1):
-        for direction in (1, -1):
-            arrived = from_behind(green_diag, "energy", direction * distance)
-            sigma_out = contribute(sigma_out, arrived, direction * distance)
-    return (green_diag, sigma_out)
+    padded = jnp.pad(energy_owner, OFFSET_MAX, constant_values=-4 * energy_count)
+    window = lax.dynamic_slice_in_dim(padded, energy_index * slot_count, slot_count + 2 * OFFSET_MAX)
+    apart = (window[None, :] - my_owner[:, None])[:, :, None]
+    matches = (apart == -mode_offsets).astype(jnp.float32) + (apart == mode_offsets).astype(jnp.float32)
+    green_diag, sigma_out = spread(jnp.sum(matches * mode_coupling, -1), green)
+    return (green_diag[None], sigma_out[None])
 
 
 def solution(mesh):

time: 97.9 us -> 82.8 us (0.85)
  the two profiles are of different devices: /device:TPU:105 before, /device:TPU:25 now
where the time goes in v2:
time: 82.8 us; the launch traced here: 82.5 us
  Pallas kernels  71.6 us (86%)
  local copies, waits for them, and re-layouts  4.43 us (5%)
  other arithmetic  3.77 us (5%)
  matrix products  2 us (2%)
    pallas_call x1, Pallas kernels, per_device(): pl.pallas_call(comp_kernel, out_shape=jax.ShapeDtypeStruct(mine.shape, jn...  30.7 us
    pallas_call x1, Pallas kernels, spread(): pl.pallas_call(spread_kernel, out_shape=(shape, shape), in_specs=[pl.Bloc...  23.7 us
    pallas_call x1, Pallas kernels, gather(): pl.pallas_call(gather_kernel, out_shape=(jax.ShapeDtypeStruct(block.shape...  17.1 us
    unnamed x10, local copies, waits for them, and re-layouts  3.66 us
    dot_general x4, matrix products, per_device(): mm = lambda x, y: jnp.matmul(x, y.T, precision=PRECISE)  2 us

profile of v2, /device:TPU:25, one launch (start us, length us, event | category | flops | bytes accessed | tf_op | source)
XLA Modules:
  0.0 82.5 jit_solution(16759780168105564421)
XLA Ops:
  0.6 0.0 copy-start
  0.7 0.8 pad_dynamic-slice_fusion
  1.4 0.7 neg.3
  2.1 0.7 multiply_add_fusion
  2.8 0.1 broadcast_subtract_fusion
  2.9 1.3 %multiply_reduce_fusion.weights_ref = f32[4,20]{1,0:T(4,128)} fusion(f32[4]{0:T(128)} %param.10, s32[4,20]{1,0:T(4,128)S(1)} %broadcast_subtract_fusion, s32[4]{0:T(128)} %param.9, s32[4]{0:T(128)S(1)} %neg.3), kind=kLoop, calls=%fused_computation.26 | loop fusion | flops 2160 | bytes 688 | tf_op jit(solution)/shard_map/reduce_sum | solution.py:417
  4.2 1.2 %fusion.5 = f32[128,128]{1,0:T(8,128)S(1)} fusion(f32[1,2,128,128]{3,2,1,0:T(8,128)} %link_ref.1), kind=kOutput, calls=%fused_computation.10 | convolution fusion | flops 25165824 | bytes 131072 | tf_op jit(solution)/shard_map/dot_general | solution.py:401
  5.4 0.0 copy-done
  5.4 0.0 copy-start.1
  5.4 0.3 fusion.2
  5.7 0.3 fusion.8
  6.0 0.3 fusion.4
  6.3 0.0 copy-start.3
  6.3 0.2 copy-done.1
  6.5 0.7 copy-done.3
  7.2 0.9 %bitcast_subtract_fusion.block_ref = f32[4,2,128,128]{3,2,1,0:T(8,128)} fusion(f32[1,4,2,128,128]{4,3,2,1,0:T(8,128)S(1)} %copy-done.1, f32[2,128,128]{2,1,0:T(8,128)S(1)} %bitcast.25, f32[2,128,128]{2,1,0:T(8,128)S(1)} %pad_maximum_fusion, f32[2,128,128]{2,1,0:T(8,128)S(1)} %pad_convert_fusion, f32[4]{0:T(128)S(1)} %get-tuple-element.10), kind=kLoop, calls=%fused_computation.7 | loop fusion | flops 524288 | bytes 1441808 | tf_op jit(solution)/shard_map/sub | solution.py:408
  8.2 17.1 %shard_map.77 = (f32[4,2,128,128]{3,2,1,0:T(8,128)}, f32[3,2,128,128]{3,2,1,0:T(8,128)}) custom-call(f32[4,2,128,128]{3,2,1,0:T(8,128)} %bitcast_subtract_fusion.block_ref, f32[1,2,128,128]{3,2,1,0:T(8,128)} %link_ref.1), custom_call_target="tpu_custom_call" | custom-call | tf_op jit(solution)/shard_map/pallas_call | solution.py:357
  25.3 30.7 %shard_map.78.green_ref = f32[4,2,128,128]{3,2,1,0:T(8,128)} custom-call(f32[4,2,128,128]{3,2,1,0:T(8,128)} %get-tuple-element.6.a_ref, f32[3,2,128,128]{3,2,1,0:T(8,128)} %get-tuple-element.7.v_ref), custom_call_target="tpu_custom_call" | custom-call | tf_op jit(solution)/shard_map/pallas_call | solution.py:410
  56.0 23.7 %shard_map.79 = (f32[4,2,128,128]{3,2,1,0:T(8,128)}, f32[4,2,128,128]{3,2,1,0:T(8,128)}) custom-call(f32[4,20]{1,0:T(4,128)} %multiply_reduce_fusion.weights_ref, f32[4,2,128,128]{3,2,1,0:T(8,128)} %shard_map.78.green_ref), custom_call_target="tpu_custom_call" | custom-call | tf_op jit(solution)/shard_map/pallas_call | solution.py:374
  79.7 0.0 copy-start.2
  79.7 1.9 %copy.10 = f32[1,4,2,128,128]{4,3,2,1,0:T(8,128)} copy(f32[1,4,2,128,128]{4,3,2,1,0:T(8,128)} %bitcast.24) | data formatting | bytes 1048576
  81.7 0.0 copy-done.2
  81.7 0.8 copy.11
  (3 shorter events, 0.0 us)
Async XLA Ops:
  0.6 4.8 %copy-start = (f32[1,2,128,128]{3,2,1,0:T(8,128)S(1)}, f32[1,2,128,128]{3,2,1,0:T(8,128)}, u32[]{:S(2)}) copy-start(f32[1,2,128,128]{3,2,1,0:T(8,128)} %link_ref.1) | copy-start | bytes 393220
  5.4 1.0 %copy-start.1 = (f32[1,4,2,128,128]{4,3,2,1,0:T(8,128)S(1)}, f32[1,4,2,128,128]{4,3,2,1,0:T(8,128)}, u32[]{:S(2)}) copy-start(f32[1,4,2,128,128]{4,3,2,1,0:T(8,128)} %param.8) | copy-start | bytes 1572868
  6.3 0.9 %copy-start.3 = (f32[1,2,128,128]{3,2,1,0:T(8,128)S(1)}, f32[1,2,128,128]{3,2,1,0:T(8,128)}, u32[]{:S(2)}) copy-start(f32[1,2,128,128]{3,2,1,0:T(8,128)} %param.6) | copy-start | bytes 393220
  79.7 1.9 %copy-start.2 = (f32[4,2,128,128]{3,2,1,0:T(8,128)S(1)}, f32[4,2,128,128]{3,2,1,0:T(8,128)}, u32[]{:S(2)}) copy-start(f32[4,2,128,128]{3,2,1,0:T(8,128)} %get-tuple-element.9) | copy-start | bytes 1572868

commit v3 on v2

--- a/solution.py
+++ b/solution.py
@@ -116,28 +116,24 @@
 def add(x, y): return x[0] + y[0], x[1] + y[1]
 def sub(x, y): return x[0] - y[0], x[1] - y[1]
 
-def solve(a, v):
-    v0, v1, v2 = v
-    h0, h1, h2 = adj(v0), adj(v1), adj(v2)
-    g0, g3 = invert_all([a[0], a[3]])
+def solve(block, link, keep):
+    g0, g3 = invert_all([block(0), block(3)])
+    v0, v2 = link(0), link(2)
+    h0, h2 = adj(v0), adj(v2)
     t0 = cprod(g0, v0)
-    d1 = sub(a[1], cprod(h0, t0))
     u3 = cprod(g3, h2)
-    d2 = sub(a[2], cprod(v2, u3))
+    d2 = sub(block(2), cprod(v2, u3))
     g2, = invert_all([d2])
-    w = cprod(g2, h1)
+    d1 = sub(block(1), cprod(h0, t0))
+    v1 = link(1)
+    w = cprod(g2, adj(v1))
     green1, = invert_all([sub(d1, cprod(v1, w))])
+    keep(1, green1)
     green2 = add(g2, cprod(w, cprod(green1, cprod(v1, g2))))
-    green0 = add(g0, cprod(t0, cprod(green1, cprod(h0, g0))))
-    green3 = add(g3, cprod(u3, cprod(green2, cprod(v2, g3))))
-    return green0, green1, green2, green3
-
-def comp_kernel(a_ref, v_ref, g_ref):
-    a = [(a_ref[c, 0], a_ref[c, 1]) for c in range(4)]
-    v = [(v_ref[c, 0], v_ref[c, 1]) for c in range(3)]
-    for c, g in enumerate(solve(a, v)):
-        g_ref[c, 0] = g[0]
-        g_ref[c, 1] = g[1]
+    keep(2, green2)
+    keep(0, add(g0, cprod(t0, cprod(green1, cprod(h0, g0)))))
+    keep(3, add(g3, cprod(u3, cprod(green2, cprod(v2, g3)))))
+
 
 MESH = pl.DeviceIdType.MESH
 ARRIVALS = (1, 3, 2)
@@ -150,21 +146,47 @@
     )
 
 
-def gather_kernel(block_ref, link_ref, mine_ref, links_ref, a_sent, a_landed, v_sent, v_landed):
-    cells = 4
+def chain_kernel(owner_ref, ham_ref, link_ref, self_ref, green_ref, sends, mine, links, fold,
+                 a_sent, a_landed, v_sent, v_landed):
+    cells, slots = 4, 4
     me = lax.axis_index("cell")
+    energy = lax.axis_index("energy")
+    last = slots * lax.axis_size("energy") - 1
     other = lambda distance: lax.rem(me + distance, cells)
     barrier = pltpu.get_barrier_semaphore()
     for distance in ARRIVALS:
         pl.semaphore_signal(barrier, 1, device_id={"cell": other(distance)}, device_id_type=MESH)
+    side = fold.shape[-1]
+    eye = jnp.where(
+        lax.broadcasted_iota(jnp.int32, (side, side), 0) == lax.broadcasted_iota(jnp.int32, (side, side), 1), 1.0, 0.0)
+    at_start = jnp.where(me == 0, CONTACT_RATE, 0.0)
+    fold[0] = -ham_ref[0, 0]
+    fold[1] = (BROADENING + at_start) * eye - ham_ref[0, 1]
+
+    @pl.when(me == cells - 1)
+    def _():
+        link = link_ref[0, 0], link_ref[0, 1]
+        beyond = cprod(link, adj(link))
+        fold[0] = fold[0] - LEAD_WIDTH * beyond[1]
+        fold[1] = fold[1] + LEAD_WIDTH * beyond[0]
+
+    def make(slot, target, at):
+        index = jnp.full((1, side), owner_ref[slots * energy + slot], jnp.int32)
+        level = BAND_LOW + BAND_SPAN * index.astype(jnp.float32) / last
+        target[at, 0] = level * eye + fold[0] - self_ref[0, slot, 0]
+        target[at, 1] = fold[1] - self_ref[0, slot, 1]
+
+    for distance in ARRIVALS:
+        make(other(distance), sends, distance - 1)
+    make(me, mine, me)
     pl.semaphore_wait(barrier, cells - 1)
 
     def a_copy(distance, owner):
-        return remote(block_ref.at[other(distance)], mine_ref.at[owner], a_sent.at[distance - 1],
+        return remote(sends.at[distance - 1], mine.at[owner], a_sent.at[distance - 1],
                       a_landed.at[owner], {"cell": other(distance)})
 
     def v_copy(distance, owner):
-        return remote(link_ref.at[0], links_ref.at[owner], v_sent.at[distance - 1],
+        return remote(link_ref.at[0], links.at[owner], v_sent.at[distance - 1],
                       v_landed.at[owner], {"cell": other(distance)})
 
     for distance in ARRIVALS:
@@ -174,15 +196,25 @@
     def _():
         for distance in ARRIVALS:
             v_copy(distance, me).start()
-        links_ref[me] = link_ref[0]
-
-    mine_ref[me] = block_ref[me]
-    for distance in ARRIVALS:
-        a_copy(distance, other(cells - distance)).wait_recv()
-
-        @pl.when(other(cells - distance) < cells - 1)
-        def _():
-            v_copy(distance, other(cells - distance)).wait_recv()
+        links[me] = link_ref[0]
+
+    def wait_a(cell):
+        @pl.when(me != cell)
+        def _():
+            a_copy(1, cell).wait_recv()
+        return mine[cell, 0], mine[cell, 1]
+
+    def wait_v(cell):
+        @pl.when(me != cell)
+        def _():
+            v_copy(1, cell).wait_recv()
+        return links[cell, 0], links[cell, 1]
+
+    def keep(cell, green):
+        green_ref[cell, 0] = green[0]
+        green_ref[cell, 1] = green[1]
+
+    solve(wait_a, wait_v, keep)
     for distance in ARRIVALS:
         a_copy(distance, me).wait_send()
 
@@ -192,7 +224,7 @@
             v_copy(distance, me).wait_send()
 
 
-def spread_kernel(weights_ref, green_ref, diag_ref, sigma_ref, near, x_sent, x_landed, z_sent, f_sent, landed):
+def spread_kernel(owner_ref, offsets_ref, strengths_ref, green_ref, diag_ref, sigma_ref, near, weights, x_sent, x_landed, z_sent, f_sent, landed):
     cells = 4
     me = lax.axis_index("cell")
     energy = lax.axis_index("energy")
@@ -295,9 +327,9 @@
         slot = from_slot(step)
         blocks = [near[0, slot], near[1, slot], diag_ref[slot], near[2, slot], near[3, slot]]
         for q in range(4):
-            total = weights_ref[q, slot] * blocks[0]
+            total = weights[q, step] * blocks[0]
             for o in range(1, 5):
-                total += weights_ref[q, 4 * o + slot] * blocks[o]
+                total += weights[q, 4 * o + step] * blocks[o]
             sigma_ref[q] = total if step == 0 else sigma_ref[q] + total
 
     send(0)
@@ -319,6 +351,17 @@
         @pl.when(core == 1)
         def _():
             near[2] = zero
+
+    def weigh(q, o, step):
+        place = jnp.clip(4 * (energy + o - 2) + from_slot(step), 0, 4 * energies - 1)
+        apart = jnp.abs(owner_ref[place] - owner_ref[4 * energy + q])
+        terms = [jnp.where(apart == offsets_ref[m], strengths_ref[m], 0.0) for m in range(4)]
+        weights[q, 4 * o + step] = (terms[0] + terms[1]) + (terms[2] + terms[3])
+
+    for q in range(4):
+        for o in range(5):
+            for step in range(4):
+                weigh(q, o, step)
     receive_x(1)
     receive_x(2)
     relay(0)
@@ -351,70 +394,45 @@
             forward(step, 3, 2).wait_send()
 
 
-def gather(block, links):
+def chain(owner, hamiltonian, coupling, sigma_in):
     vmem = pl.BlockSpec(memory_space=pltpu.VMEM)
     dma = pltpu.SemaphoreType.DMA
+    shape = sigma_in.shape[1:]
+    buffer = lambda count: pltpu.VMEM((count,) + shape[1:], jnp.float32)
     return pl.pallas_call(
-        gather_kernel,
-        out_shape=(
-            jax.ShapeDtypeStruct(block.shape, jnp.float32),
-            jax.ShapeDtypeStruct((3,) + block.shape[1:], jnp.float32),
-        ),
-        in_specs=[vmem, vmem],
-        out_specs=(vmem, vmem),
-        scratch_shapes=[dma((3,)), dma((4,)), dma((3,)), dma((3,))],
+        chain_kernel,
+        out_shape=jax.ShapeDtypeStruct(shape, jnp.float32),
+        in_specs=[pl.BlockSpec(memory_space=pltpu.SMEM), vmem, vmem, vmem],
+        out_specs=vmem,
+        scratch_shapes=[
+            buffer(3), buffer(4), buffer(3), pltpu.VMEM(shape[1:], jnp.float32),
+            dma((3,)), dma((4,)), dma((3,)), dma((3,)),
+        ],
         compiler_params=pltpu.CompilerParams(collective_id=0, has_side_effects=True),
-    )(block, links)
-
-
-def spread(weights, green):
+    )(owner, hamiltonian, coupling, sigma_in)
+
+
+def spread(owner, offsets, strengths, green):
     vmem = pl.BlockSpec(memory_space=pltpu.VMEM)
     dma = pltpu.SemaphoreType.DMA
     shape = jax.ShapeDtypeStruct(green.shape, jnp.float32)
     return pl.pallas_call(
         spread_kernel,
         out_shape=(shape, shape),
-        in_specs=[pl.BlockSpec(memory_space=pltpu.SMEM), vmem],
+        in_specs=[pl.BlockSpec(memory_space=pltpu.SMEM)] * 3 + [vmem],
         out_specs=(vmem, vmem),
         scratch_shapes=[
             pltpu.VMEM((4,) + green.shape, jnp.float32),
+            pltpu.SMEM((4, 20), jnp.float32),
             dma((3,)), dma((4,)), dma((3, 4)), dma((4,)), dma((4, 4)),
         ],
         compiler_params=pltpu.CompilerParams(collective_id=1, has_side_effects=True),
-    )(weights, green)
+    )(owner, offsets, strengths, green)
 
 
 def per_device(hamiltonian, coupling, sigma_in, mode_offsets, mode_coupling, energy_owner):
-    slot_count = sigma_in.shape[1]
-    orbitals = hamiltonian.shape[-1]
-    chain_length = lax.axis_size("cell")
-    energy_devices = lax.axis_size("energy")
-    chain_index = lax.axis_index("cell")
-    energy_index = lax.axis_index("energy")
-    energy_count = slot_count * energy_devices
-    identity = jnp.eye(orbitals, dtype=jnp.float32)
-    at_start = (chain_index == 0).astype(jnp.float32)
-    at_end = (chain_index == chain_length - 1).astype(jnp.float32)
-    my_owner = lax.dynamic_slice_in_dim(energy_owner, energy_index * slot_count, slot_count)
-    energy_level = BAND_LOW + BAND_SPAN * my_owner.astype(jnp.float32) / (energy_count - 1)
-    last_r, last_i = coupling[0, 0], coupling[0, 1]
-    mm = lambda x, y: jnp.matmul(x, y.T, precision=PRECISE)
-    beyond_r = mm(last_r, last_r) + mm(last_i, last_i)
-    beyond_i = mm(last_i, last_r) - mm(last_r, last_i)
-    fold_r = -LEAD_WIDTH * at_end * beyond_i
-    fold_i = LEAD_WIDTH * at_end * beyond_r + (BROADENING + CONTACT_RATE * at_start) * identity
-    fold = jnp.stack([fold_r, fold_i])
-    level = energy_level[:, None, None, None] * jnp.stack([identity, jnp.zeros_like(identity)])[None]
-    block = level + fold[None] - hamiltonian - sigma_in[0]
-    mine, links = gather(block, coupling)
-    green = pl.pallas_call(
-        comp_kernel, out_shape=jax.ShapeDtypeStruct(mine.shape, jnp.float32)
-    )(mine, links)
-    padded = jnp.pad(energy_owner, OFFSET_MAX, constant_values=-4 * energy_count)
-    window = lax.dynamic_slice_in_dim(padded, energy_index * slot_count, slot_count + 2 * OFFSET_MAX)
-    apart = (window[None, :] - my_owner[:, None])[:, :, None]
-    matches = (apart == -mode_offsets).astype(jnp.float32) + (apart == mode_offsets).astype(jnp.float32)
-    green_diag, sigma_out = spread(jnp.sum(matches * mode_coupling, -1), green)
+    green = chain(energy_owner, hamiltonian, coupling, sigma_in)
+    green_diag, sigma_out = spread(energy_owner, mode_offsets, mode_coupling, green)
     return (green_diag[None], sigma_out[None])
 
 

time: 82.8 us -> 65.3 us (0.79)
  Pallas kernels: 71.6 us -> 61.7 us
  other arithmetic: 3.77 us -> 0 us
  matrix products: 2 us -> 0 us
  local copies, waits for them, and re-layouts: 4.43 us -> 2.73 us
    pallas_call x2 -> x1, Pallas kernels: 47.8 us -> 33.9 us  [chain(): pl.pallas_call(chain_kernel, out_shape=jax.ShapeDtypeStruct(shape, jnp.fl...]
    pallas_call x1, Pallas kernels: 23.7 us -> 27.8 us  [spread(): pl.pallas_call(spread_kernel, out_shape=(shape, shape), in_specs=[pl.Bloc...]
    dot_general x4 -> x0, matrix products: 2 us -> none  [per_device(): mm = lambda x, y: jnp.matmul(x, y.T, precision=PRECISE)]
    reduce_sum x1 -> x0, other arithmetic: 1.34 us -> none  [per_device(): green_diag, sigma_out = spread(jnp.sum(matches * mode_coupling, -1), green)]
    sub x2 -> x0, other arithmetic: 1.01 us -> none  [the longest x1 0.94 us: per_device(): block = level + fold[None] - hamiltonian - sigma_in[0]]
    unnamed x10 -> x4, local copies, waits for them, and re-layouts: 3.66 us -> 2.73 us
where the time goes in v3:
time: 65.3 us; the launch traced here: 65.1 us
  Pallas kernels  61.7 us (94%)
  local copies, waits for them, and re-layouts  2.73 us (4%)
  between operations  0.66 us (1%)
    pallas_call x1, Pallas kernels, chain(): pl.pallas_call(chain_kernel, out_shape=jax.ShapeDtypeStruct(shape, jnp.fl...  33.9 us
    pallas_call x1, Pallas kernels, spread(): pl.pallas_call(spread_kernel, out_shape=(shape, shape), in_specs=[pl.Bloc...  27.8 us
    unnamed x4, local copies, waits for them, and re-layouts  2.73 us

profile of v3, /device:TPU:25, one launch (start us, length us, event | category | flops | bytes accessed | tf_op | source)
XLA Modules:
  0.0 65.1 jit_solution(1846555075164817711)
XLA Ops:
  0.6 33.9 %shard_map.77.green_ref = f32[4,2,128,128]{3,2,1,0:T(8,128)} custom-call(s32[128]{0:T(128)} %owner_ref.3, f32[1,2,128,128]{3,2,1,0:T(8,128)} %ham_ref.1, f32[1,2,128,128]{3,2,1,0:T(8,128)} %link_ref.1, f32[1,4,2,128,128]{4,3,2,1,0:T(8,128)} %self_ref.1), custom_call_target="tpu_custom_call" | custom-call | tf_op jit(solution)/shard_map/pallas_call | solution.py:402
  34.6 27.8 %shard_map.78 = (f32[4,2,128,128]{3,2,1,0:T(8,128)}, f32[4,2,128,128]{3,2,1,0:T(8,128)}) custom-call(s32[128]{0:T(128)} %owner_ref.3, s32[4]{0:T(128)} %offsets_ref.1, f32[4]{0:T(128)} %strengths_ref.1, f32[4,2,128,128]{3,2,1,0:T(8,128)} %shard_map.77.green_ref), custom_call_target="tpu_custom_call" | custom-call | tf_op jit(solution)/shard_map/pallas_call | solution.py:419
  62.4 0.0 copy-start
  62.4 1.9 %copy.10 = f32[1,4,2,128,128]{4,3,2,1,0:T(8,128)} copy(f32[1,4,2,128,128]{4,3,2,1,0:T(8,128)} %bitcast.3) | data formatting | bytes 1048576
  64.3 0.0 copy-done
  64.3 0.8 %copy.11 = f32[1,4,2,128,128]{4,3,2,1,0:T(8,128)} copy(f32[1,4,2,128,128]{4,3,2,1,0:T(8,128)S(1)} %bitcast.2) | data formatting | bytes 1048576
Async XLA Ops:
  62.4 1.9 %copy-start = (f32[4,2,128,128]{3,2,1,0:T(8,128)S(1)}, f32[4,2,128,128]{3,2,1,0:T(8,128)}, u32[]{:S(2)}) copy-start(f32[4,2,128,128]{3,2,1,0:T(8,128)} %get-tuple-element.5) | copy-start | bytes 1572868

commit v4 on v3

--- a/solution.py
+++ b/solution.py
@@ -14,6 +14,7 @@
 BAND_LOW = -2.5
 BAND_SPAN = 5.0
 HALF = 64
+VMEM_LIMIT = 16 * 2**20
 
 
 def dot(x, y):
@@ -46,31 +47,36 @@
             for k in range(8):
                 pr, pi = wide(cr[k][k:k + 1]), wide(ci[k][k:k + 1])
                 d = 1.0 / (pr * pr + pi * pi)
-                ir, ii = pr * d, -pi * d
-                row = wide(panel[k:k + 1]) + jnp.where(li == base + k, 1.0, 0.0)
-                turn = wide(spun[k:k + 1]) + jnp.where(li == HALF + base + k, 1.0, 0.0)
-                v = ir * row + ii * turn
-                vt = ir * turn - ii * row
                 ur, ui = cr[k] - jnp.where(si == k, 1.0, 0.0), ci[k]
                 for j in range(k + 1, 8):
                     xr, xi = wide(cr[j][k:k + 1]), wide(ci[j][k:k + 1])
-                    wr = ir * xr - ii * xi
-                    wi = ir * xi + ii * xr
-                    cr[j] = cr[j] - (ur * wr - ui * wi)
-                    ci[j] = ci[j] - (ur * wi + ui * wr)
-                panel = panel - (ur * v + ui * vt)
-                spun = spun - (ur * vt - ui * v)
+                    wr = xr * pr + xi * pi
+                    wi = xi * pr - xr * pi
+                    cr[j] = cr[j] - d * (ur * wr - ui * wi)
+                    ci[j] = ci[j] - d * (ur * wi + ui * wr)
+                row = wide(panel[k:k + 1]) + jnp.where(li == base + k, 1.0, 0.0)
+                turn = wide(spun[k:k + 1]) + jnp.where(li == HALF + base + k, 1.0, 0.0)
+                v = row * pr - turn * pi
+                vt = turn * pr + row * pi
+                panel = panel - d * (ur * v + ui * vt)
+                spun = spun - d * (ur * vt - ui * v)
             full = panel + jnp.where(li == base + si, 1.0, 0.0)
             turned = spun + jnp.where(li == HALF + base + si, 1.0, 0.0)
             fr = [wide(full[j:j + 1]) for j in range(8)]
             ft = [wide(turned[j:j + 1]) for j in range(8)]
-            order = [t for t in range(g + 1, n)] + [t for t in range(g)]
-            for t in order:
+            near = [g + 1] if g + 1 < n else []
+            far = [t for t in range(g + 2, n)] + [t for t in range(g)]
+            for t in near:
                 x = rows[t]
                 terms = [wide(x[:, base + j:base + j + 1]) * fr[j] + wide(x[:, HALF + base + j:HALF + base + j + 1]) * ft[j] for j in range(8)]
                 while len(terms) > 1:
                     terms = [p + q for p, q in zip(terms[::2], terms[1::2])]
                 rows[t] = x - terms[0]
+            empty = jnp.zeros_like(full)
+            weight = jnp.concatenate([full if t == g else turned if t == g + n else empty for t in range(2 * n)], axis=0)
+            moved = dot(jnp.concatenate([rows[t] for t in far], axis=0), weight)
+            for at, t in enumerate(far):
+                rows[t] = rows[t] - moved[8 * at:8 * at + 8]
             rows[g] = panel
     return [jnp.concatenate(rows, axis=0) for rows in tiles]
 
@@ -127,12 +133,17 @@
     d1 = sub(block(1), cprod(h0, t0))
     v1 = link(1)
     w = cprod(g2, adj(v1))
+    y2 = cprod(v1, g2)
+    y0 = cprod(h0, g0)
+    x3 = cprod(v2, g3)
+    base3 = add(g3, cprod(u3, cprod(g2, x3)))
+    y3 = cprod(y2, x3)
+    w3 = cprod(u3, w)
     green1, = invert_all([sub(d1, cprod(v1, w))])
     keep(1, green1)
-    green2 = add(g2, cprod(w, cprod(green1, cprod(v1, g2))))
-    keep(2, green2)
-    keep(0, add(g0, cprod(t0, cprod(green1, cprod(h0, g0)))))
-    keep(3, add(g3, cprod(u3, cprod(green2, cprod(v2, g3)))))
+    keep(2, add(g2, cprod(w, cprod(green1, y2))))
+    keep(0, add(g0, cprod(t0, cprod(green1, y0))))
+    keep(3, add(base3, cprod(w3, cprod(green1, y3))))
 
 
 MESH = pl.DeviceIdType.MESH
@@ -146,8 +157,15 @@
     )
 
 
-def chain_kernel(owner_ref, ham_ref, link_ref, self_ref, green_ref, sends, mine, links, fold,
-                 a_sent, a_landed, v_sent, v_landed):
+def chain_kernel(owner_hbm, ham_hbm, link_hbm, self_hbm, green_ref, owner_ref, ham_ref, link_ref, self_ref,
+                 sends, mine, links, fold, loaded, a_sent, a_landed, v_sent, v_landed):
+    loads = [
+        pltpu.make_async_copy(source, target, loaded.at[at])
+        for at, (source, target) in enumerate(
+            ((owner_hbm, owner_ref), (ham_hbm, ham_ref), (link_hbm, link_ref), (self_hbm, self_ref)))
+    ]
+    for load in loads:
+        load.start()
     cells, slots = 4, 4
     me = lax.axis_index("cell")
     energy = lax.axis_index("energy")
@@ -160,6 +178,8 @@
     eye = jnp.where(
         lax.broadcasted_iota(jnp.int32, (side, side), 0) == lax.broadcasted_iota(jnp.int32, (side, side), 1), 1.0, 0.0)
     at_start = jnp.where(me == 0, CONTACT_RATE, 0.0)
+    for load in loads:
+        load.wait()
     fold[0] = -ham_ref[0, 0]
     fold[1] = (BROADENING + at_start) * eye - ham_ref[0, 1]
 
@@ -402,11 +422,15 @@
     return pl.pallas_call(
         chain_kernel,
         out_shape=jax.ShapeDtypeStruct(shape, jnp.float32),
-        in_specs=[pl.BlockSpec(memory_space=pltpu.SMEM), vmem, vmem, vmem],
+        in_specs=[pl.BlockSpec(memory_space=pltpu.HBM)] * 4,
         out_specs=vmem,
         scratch_shapes=[
+            pltpu.SMEM(owner.shape, jnp.int32),
+            pltpu.VMEM(hamiltonian.shape, jnp.float32),
+            pltpu.VMEM(coupling.shape, jnp.float32),
+            pltpu.VMEM(sigma_in.shape, jnp.float32),
             buffer(3), buffer(4), buffer(3), pltpu.VMEM(shape[1:], jnp.float32),
-            dma((3,)), dma((4,)), dma((3,)), dma((3,)),
+            dma((4,)), dma((3,)), dma((4,)), dma((3,)), dma((3,)),
         ],
         compiler_params=pltpu.CompilerParams(collective_id=0, has_side_effects=True),
     )(owner, hamiltonian, coupling, sigma_in)
@@ -426,13 +450,36 @@
             pltpu.SMEM((4, 20), jnp.float32),
             dma((3,)), dma((4,)), dma((3, 4)), dma((4,)), dma((4, 4)),
         ],
-        compiler_params=pltpu.CompilerParams(collective_id=1, has_side_effects=True),
+        compiler_params=pltpu.CompilerParams(collective_id=1, has_side_effects=True, vmem_limit_bytes=VMEM_LIMIT),
     )(owner, offsets, strengths, green)
+
+
+def write_kernel(diag_ref, sigma_ref, diag_out, sigma_out, done):
+    copies = [
+        pltpu.make_async_copy(diag_ref, diag_out, done.at[0]),
+        pltpu.make_async_copy(sigma_ref, sigma_out, done.at[1]),
+    ]
+    for copy in copies:
+        copy.start()
+    for copy in copies:
+        copy.wait()
+
+
+def write(diag, sigma):
+    shape = jax.ShapeDtypeStruct(diag.shape, jnp.float32)
+    return pl.pallas_call(
+        write_kernel,
+        out_shape=(shape, shape),
+        in_specs=[pl.BlockSpec(memory_space=pltpu.VMEM)] * 2,
+        out_specs=(pl.BlockSpec(memory_space=pl.ANY),) * 2,
+        scratch_shapes=[pltpu.SemaphoreType.DMA((2,))],
+        compiler_params=pltpu.CompilerParams(vmem_limit_bytes=VMEM_LIMIT),
+    )(diag, sigma)
 
 
 def per_device(hamiltonian, coupling, sigma_in, mode_offsets, mode_coupling, energy_owner):
     green = chain(energy_owner, hamiltonian, coupling, sigma_in)
-    green_diag, sigma_out = spread(energy_owner, mode_offsets, mode_coupling, green)
+    green_diag, sigma_out = write(*spread(energy_owner, mode_offsets, mode_coupling, green))
     return (green_diag[None], sigma_out[None])
 
 

time: 65.3 us -> 59.6 us (0.913)
  Pallas kernels: 61.7 us -> 57.5 us
  local copies, waits for them, and re-layouts: 2.73 us -> 1.05 us
    pallas_call x1, Pallas kernels: 27.8 us -> 24.7 us  [spread(): pl.pallas_call(spread_kernel, out_shape=(shape, shape), in_specs=[pl.Bloc...]
    pallas_call x1, Pallas kernels: 33.9 us -> 31.8 us  [chain(): pl.pallas_call(chain_kernel, out_shape=jax.ShapeDtypeStruct(shape, jnp.fl...]
    unnamed x4 -> x8, local copies, waits for them, and re-layouts: 2.73 us -> 1.05 us
    pallas_call x0 -> x1, Pallas kernels: none -> 0.99 us  [write(): pl.pallas_call(write_kernel, out_shape=(shape, shape), in_specs=[pl.Block...]
where the time goes in v4:
time: 59.6 us; the launch traced here: 59.4 us
  Pallas kernels  57.5 us (96%)
  local copies, waits for them, and re-layouts  1.05 us (2%)
  between operations  0.86 us (1%)
    pallas_call x1, Pallas kernels, chain(): pl.pallas_call(chain_kernel, out_shape=jax.ShapeDtypeStruct(shape, jnp.fl...  31.8 us
    pallas_call x1, Pallas kernels, spread(): pl.pallas_call(spread_kernel, out_shape=(shape, shape), in_specs=[pl.Bloc...  24.7 us

profile of v4, /device:TPU:25, one launch (start us, length us, event | category | flops | bytes accessed | tf_op | source)
XLA Modules:
  0.0 59.4 jit_solution(7255072450630204446)
XLA Ops:
  0.6 0.0 copy-start.1
  0.6 0.0 copy-start.3
  0.7 0.0 copy-start.2
  0.7 31.8 %shard_map.77.green_ref = f32[4,2,128,128]{3,2,1,0:T(8,128)} custom-call(s32[128]{0:T(128)} %owner_ref.1, f32[1,2,128,128]{3,2,1,0:T(8,128)} %ham_hbm.1, f32[1,2,128,128]{3,2,1,0:T(8,128)} %link_hbm.1, f32[1,4,2,128,128]{4,3,2,1,0:T(8,128)} %self_hbm.1), custom_call_target="tpu_custom_call" | custom-call | tf_op jit(solution)/shard_map/pallas_call | solution.py:422
  32.5 0.0 copy-done.1
  32.5 0.0 copy-done.3
  32.5 0.0 copy-done.2
  32.5 0.0 copy-start
  32.5 1.0 %copy-done = f32[4,2,128,128]{3,2,1,0:T(8,128)S(1)} copy-done((f32[4,2,128,128]{3,2,1,0:T(8,128)S(1)}, f32[4,2,128,128]{3,2,1,0:T(8,128)}, u32[]{:S(2)}) %copy-start) | copy-done | bytes 524312
  33.6 24.7 %shard_map.78 = (f32[4,2,128,128]{3,2,1,0:T(8,128)S(1)}, f32[4,2,128,128]{3,2,1,0:T(8,128)S(1)}) custom-call(s32[128]{0:T(128)S(1)} %copy-done.1, s32[4]{0:T(128)S(1)} %copy-done.2, f32[4]{0:T(128)S(1)} %copy-done.3, f32[4,2,128,128]{3,2,1,0:T(8,128)S(1)} %copy-done), custom_call_target="tpu_custom_call" | custom-call | tf_op jit(solution)/shard_map/pallas_call | solution.py:443
  58.3 1.0 %shard_map.79 = (f32[4,2,128,128]{3,2,1,0:T(8,128)}, f32[4,2,128,128]{3,2,1,0:T(8,128)}) custom-call(f32[4,2,128,128]{3,2,1,0:T(8,128)S(1)} %get-tuple-element.6.diag_ref, f32[4,2,128,128]{3,2,1,0:T(8,128)S(1)} %get-tuple-element.7.sigma_ref), custom_call_target="tpu_custom_call" | custom-call | tf_op jit(solution)/shard_map/pallas_call | solution.py:470
Async XLA Ops:
  0.6 31.9 %copy-start.1 = (s32[128]{0:T(128)S(1)}, s32[128]{0:T(128)}, u32[]{:S(2)}) copy-start(s32[128]{0:T(128)} %owner_ref.1) | copy-start | bytes 1540
  0.6 31.9 %copy-start.3 = (f32[4]{0:T(128)S(1)}, f32[4]{0:T(128)}, u32[]{:S(2)}) copy-start(f32[4]{0:T(128)} %strengths_ref.1) | copy-start | bytes 52
  0.7 31.9 %copy-start.2 = (s32[4]{0:T(128)S(1)}, s32[4]{0:T(128)}, u32[]{:S(2)}) copy-start(s32[4]{0:T(128)} %offsets_ref.1) | copy-start | bytes 52
  32.5 1.0 %copy-start = (f32[4,2,128,128]{3,2,1,0:T(8,128)S(1)}, f32[4,2,128,128]{3,2,1,0:T(8,128)}, u32[]{:S(2)}) copy-start(f32[4,2,128,128]{3,2,1,0:T(8,128)} %shard_map.77.green_ref) | copy-start | bytes 1572868

commit v5 on v4

--- a/solution.py
+++ b/solution.py
@@ -14,7 +14,6 @@
 BAND_LOW = -2.5
 BAND_SPAN = 5.0
 HALF = 64
-VMEM_LIMIT = 16 * 2**20
 
 
 def dot(x, y):
@@ -157,23 +156,42 @@
     )
 
 
-def chain_kernel(owner_hbm, ham_hbm, link_hbm, self_hbm, green_ref, owner_ref, ham_ref, link_ref, self_ref,
-                 sends, mine, links, fold, loaded, a_sent, a_landed, v_sent, v_landed):
+def born_kernel(owner_hbm, ham_hbm, link_hbm, self_hbm, offsets_hbm, strengths_hbm, diag_out, sigma_out,
+                diag_ref, sigma_ref, owner_ref, ham_ref, link_ref, self_ref, offsets_ref, strengths_ref, sends, mine, links, fold,
+                green_ref, near, weights, loaded, a_sent, a_landed, v_sent, v_landed,
+                x_sent, x_landed, z_sent, f_sent, landed, stored):
     loads = [
         pltpu.make_async_copy(source, target, loaded.at[at])
         for at, (source, target) in enumerate(
-            ((owner_hbm, owner_ref), (ham_hbm, ham_ref), (link_hbm, link_ref), (self_hbm, self_ref)))
+            ((owner_hbm, owner_ref), (ham_hbm, ham_ref), (link_hbm, link_ref), (self_hbm, self_ref),
+             (offsets_hbm, offsets_ref), (strengths_hbm, strengths_ref)))
     ]
     for load in loads:
         load.start()
     cells, slots = 4, 4
     me = lax.axis_index("cell")
     energy = lax.axis_index("energy")
-    last = slots * lax.axis_size("energy") - 1
+    energies = lax.axis_size("energy")
+    last = slots * energies - 1
+    core = lax.rem(energy, 2)
+    partner = energy + 1 - 2 * core
+    lower, upper = energy >= 2, energy < energies - 2
     other = lambda distance: lax.rem(me + distance, cells)
     barrier = pltpu.get_barrier_semaphore()
+    def greet(where):
+        pl.semaphore_signal(barrier, 1, device_id=where, device_id_type=MESH)
+
     for distance in ARRIVALS:
-        pl.semaphore_signal(barrier, 1, device_id={"cell": other(distance)}, device_id_type=MESH)
+        greet({"cell": other(distance)})
+    greet({"energy": partner})
+
+    @pl.when(lower)
+    def _():
+        greet({"energy": energy - 2})
+
+    @pl.when(upper)
+    def _():
+        greet({"energy": energy + 2})
     side = fold.shape[-1]
     eye = jnp.where(
         lax.broadcasted_iota(jnp.int32, (side, side), 0) == lax.broadcasted_iota(jnp.int32, (side, side), 1), 1.0, 0.0)
@@ -199,7 +217,7 @@
     for distance in ARRIVALS:
         make(other(distance), sends, distance - 1)
     make(me, mine, me)
-    pl.semaphore_wait(barrier, cells - 1)
+    pl.semaphore_wait(barrier, cells + lower.astype(jnp.int32) + upper.astype(jnp.int32))
 
     def a_copy(distance, owner):
         return remote(sends.at[distance - 1], mine.at[owner], a_sent.at[distance - 1],
@@ -230,46 +248,17 @@
             v_copy(1, cell).wait_recv()
         return links[cell, 0], links[cell, 1]
 
+    def x_send(cell):
+        return remote(green_ref.at[cell], diag_ref.at[me], x_sent.at[cell], x_landed.at[me], {"cell": cell})
+
     def keep(cell, green):
         green_ref[cell, 0] = green[0]
         green_ref[cell, 1] = green[1]
 
-    solve(wait_a, wait_v, keep)
-    for distance in ARRIVALS:
-        a_copy(distance, me).wait_send()
-
-    @pl.when(me < cells - 1)
-    def _():
-        for distance in ARRIVALS:
-            v_copy(distance, me).wait_send()
-
-
-def spread_kernel(owner_ref, offsets_ref, strengths_ref, green_ref, diag_ref, sigma_ref, near, weights, x_sent, x_landed, z_sent, f_sent, landed):
-    cells = 4
-    me = lax.axis_index("cell")
-    energy = lax.axis_index("energy")
-    energies = lax.axis_size("energy")
-    core = lax.rem(energy, 2)
-    partner = energy + 1 - 2 * core
-    lower, upper = energy >= 2, energy < energies - 2
-    other = lambda distance: lax.rem(me + distance, cells)
-    barrier = pltpu.get_barrier_semaphore()
-
-    def greet(where):
-        pl.semaphore_signal(barrier, 1, device_id=where, device_id_type=MESH)
-
-    for distance in ARRIVALS:
-        greet({"cell": other(distance)})
-    greet({"energy": partner})
-
-    @pl.when(lower)
-    def _():
-        greet({"energy": energy - 2})
-
-    @pl.when(upper)
-    def _():
-        greet({"energy": energy + 2})
-    pl.semaphore_wait(barrier, cells + lower.astype(jnp.int32) + upper.astype(jnp.int32))
+    def ship(cell):
+        @pl.when(me != cell)
+        def _():
+            x_send(cell).start()
 
     def x_copy(distance, slot):
         return remote(green_ref.at[other(distance)], diag_ref.at[slot], x_sent.at[distance - 1],
@@ -300,9 +289,6 @@
     def arrived(side, step):
         slot = from_slot(step)
         remote(near.at[side, slot], near.at[side, slot], f_sent.at[step], landed.at[side, slot], {"energy": partner}).wait_recv()
-
-    for distance in ARRIVALS:
-        x_copy(distance, me).start()
 
     def send(step):
         @pl.when(upper)
@@ -352,8 +338,6 @@
                 total += weights[q, 4 * o + step] * blocks[o]
             sigma_ref[q] = total if step == 0 else sigma_ref[q] + total
 
-    send(0)
-    diag_ref[me] = green_ref[me]
     zero = jnp.zeros(near.shape[1:], jnp.float32)
 
     @pl.when(jnp.logical_not(lower))
@@ -382,10 +366,17 @@
         for o in range(5):
             for step in range(4):
                 weigh(q, o, step)
+    solve(wait_a, wait_v, keep)
+    for cell in (1, 2, 0, 3):
+        ship(cell)
+    send(0)
+    diag_ref[me] = green_ref[me]
     receive_x(1)
     receive_x(2)
     relay(0)
     receive_x(3)
+    stores = [pltpu.make_async_copy(diag_ref, diag_out, stored.at[0])]
+    stores[0].start()
     relay(1)
     finish(0)
     relay(2)
@@ -393,8 +384,12 @@
     relay(3)
     finish(2)
     finish(3)
-    for distance in ARRIVALS:
-        x_copy(distance, me).wait_send()
+    stores.append(pltpu.make_async_copy(sigma_ref, sigma_out, stored.at[1]))
+    stores[1].start()
+    for cell in range(4):
+        @pl.when(me != cell)
+        def _():
+            x_send(cell).wait_send()
     for step in range(4):
         @pl.when(upper)
         def _():
@@ -412,56 +407,50 @@
         @pl.when(jnp.logical_and(core == 0, upper))
         def _():
             forward(step, 3, 2).wait_send()
-
-
-def chain(owner, hamiltonian, coupling, sigma_in):
-    vmem = pl.BlockSpec(memory_space=pltpu.VMEM)
+    for distance in ARRIVALS:
+        a_copy(distance, me).wait_send()
+
+    @pl.when(me < cells - 1)
+    def _():
+        for distance in ARRIVALS:
+            v_copy(distance, me).wait_send()
+    for store in stores:
+        store.wait()
+
+
+def born(owner, hamiltonian, coupling, sigma_in, offsets, strengths):
     dma = pltpu.SemaphoreType.DMA
     shape = sigma_in.shape[1:]
+    out = jax.ShapeDtypeStruct(shape, jnp.float32)
     buffer = lambda count: pltpu.VMEM((count,) + shape[1:], jnp.float32)
+    whole = lambda x: pltpu.VMEM(x.shape, jnp.float32)
     return pl.pallas_call(
-        chain_kernel,
-        out_shape=jax.ShapeDtypeStruct(shape, jnp.float32),
-        in_specs=[pl.BlockSpec(memory_space=pltpu.HBM)] * 4,
-        out_specs=vmem,
+        born_kernel,
+        out_shape=(out, out),
+        in_specs=[pl.BlockSpec(memory_space=pltpu.HBM)] * 6,
+        out_specs=(pl.BlockSpec(memory_space=pl.ANY),) * 2,
         scratch_shapes=[
-            pltpu.SMEM(owner.shape, jnp.int32),
-            pltpu.VMEM(hamiltonian.shape, jnp.float32),
-            pltpu.VMEM(coupling.shape, jnp.float32),
-            pltpu.VMEM(sigma_in.shape, jnp.float32),
+            buffer(4), buffer(4), pltpu.SMEM(owner.shape, jnp.int32), whole(hamiltonian), whole(coupling), whole(sigma_in),
+            pltpu.SMEM(offsets.shape, jnp.int32), pltpu.SMEM(strengths.shape, jnp.float32),
             buffer(3), buffer(4), buffer(3), pltpu.VMEM(shape[1:], jnp.float32),
-            dma((4,)), dma((3,)), dma((4,)), dma((3,)), dma((3,)),
+            buffer(4), pltpu.VMEM((4,) + shape, jnp.float32), pltpu.SMEM((4, 20), jnp.float32),
+            dma((6,)), dma((3,)), dma((4,)), dma((3,)), dma((3,)),
+            dma((4,)), dma((4,)), dma((3, 4)), dma((4,)), dma((4, 4)), dma((2,)),
         ],
         compiler_params=pltpu.CompilerParams(collective_id=0, has_side_effects=True),
-    )(owner, hamiltonian, coupling, sigma_in)
-
-
-def spread(owner, offsets, strengths, green):
-    vmem = pl.BlockSpec(memory_space=pltpu.VMEM)
-    dma = pltpu.SemaphoreType.DMA
-    shape = jax.ShapeDtypeStruct(green.shape, jnp.float32)
-    return pl.pallas_call(
-        spread_kernel,
-        out_shape=(shape, shape),
-        in_specs=[pl.BlockSpec(memory_space=pltpu.SMEM)] * 3 + [vmem],
-        out_specs=(vmem, vmem),
-        scratch_shapes=[
-            pltpu.VMEM((4,) + green.shape, jnp.float32),
-            pltpu.SMEM((4, 20), jnp.float32),
-            dma((3,)), dma((4,)), dma((3, 4)), dma((4,)), dma((4, 4)),
-        ],
-        compiler_params=pltpu.CompilerParams(collective_id=1, has_side_effects=True, vmem_limit_bytes=VMEM_LIMIT),
-    )(owner, offsets, strengths, green)
-
-
-def write_kernel(diag_ref, sigma_ref, diag_out, sigma_out, done):
-    copies = [
-        pltpu.make_async_copy(diag_ref, diag_out, done.at[0]),
-        pltpu.make_async_copy(sigma_ref, sigma_out, done.at[1]),
-    ]
-    for copy in copies:
+    )(owner, hamiltonian, coupling, sigma_in, offsets, strengths)
+
+
+def write_kernel(diag_ref, sigma_ref, diag_out, sigma_out, held, read, written):
+    pairs = [(source.at[slot], target.at[slot]) for source, target in ((diag_ref, diag_out), (sigma_ref, sigma_out)) for slot in range(4)]
+    reads = [pltpu.make_async_copy(source, held.at[at], read.at[at]) for at, (source, target) in enumerate(pairs)]
+    writes = [pltpu.make_async_copy(held.at[at], target, written.at[at]) for at, (source, target) in enumerate(pairs)]
+    for copy in reads:
         copy.start()
-    for copy in copies:
+    for copy, onward in zip(reads, writes):
+        copy.wait()
+        onward.start()
+    for copy in writes:
         copy.wait()
 
 
@@ -470,16 +459,18 @@
     return pl.pallas_call(
         write_kernel,
         out_shape=(shape, shape),
-        in_specs=[pl.BlockSpec(memory_space=pltpu.VMEM)] * 2,
+        in_specs=[pl.BlockSpec(memory_space=pl.ANY)] * 2,
         out_specs=(pl.BlockSpec(memory_space=pl.ANY),) * 2,
-        scratch_shapes=[pltpu.SemaphoreType.DMA((2,))],
-        compiler_params=pltpu.CompilerParams(vmem_limit_bytes=VMEM_LIMIT),
+        scratch_shapes=[
+            pltpu.VMEM((8,) + diag.shape[1:], jnp.float32),
+            pltpu.SemaphoreType.DMA((8,)), pltpu.SemaphoreType.DMA((8,)),
+        ],
     )(diag, sigma)
 
 
 def per_device(hamiltonian, coupling, sigma_in, mode_offsets, mode_coupling, energy_owner):
-    green = chain(energy_owner, hamiltonian, coupling, sigma_in)
-    green_diag, sigma_out = write(*spread(energy_owner, mode_offsets, mode_coupling, green))
+    green_diag, sigma_out = write(
+        *born(energy_owner, hamiltonian, coupling, sigma_in, mode_offsets, mode_coupling))
     return (green_diag[None], sigma_out[None])
 
 

time: 59.6 us -> 58 us (0.973)
  the two profiles are of different devices: /device:TPU:25 before, /device:TPU:29 now
where the time goes in v5:
time: 58 us; the launch traced here: 57.8 us
  Pallas kernels  57 us (98%)
  between operations  0.8 us (1%)
    pallas_call x1, Pallas kernels, born(): pl.pallas_call(born_kernel, out_shape=(out, out), in_specs=[pl.BlockSpec(...  54.9 us
    pallas_call x1, Pallas kernels, write(): pl.pallas_call(write_kernel, out_shape=(shape, shape), in_specs=[pl.Block...  2.09 us

profile of v5, /device:TPU:29, one launch (start us, length us, event | category | flops | bytes accessed | tf_op | source)
XLA Modules:
  0.0 57.8 jit_solution(4902312547998890593)
XLA Ops:
  0.6 54.9 %shard_map.77 = (f32[4,2,128,128]{3,2,1,0:T(8,128)}, f32[4,2,128,128]{3,2,1,0:T(8,128)}) custom-call(s32[128]{0:T(128)} %owner_hbm.1, f32[1,2,128,128]{3,2,1,0:T(8,128)} %ham_hbm.1, f32[1,2,128,128]{3,2,1,0:T(8,128)} %link_hbm.1, f32[1,4,2,128,128]{4,3,2,1,0:T(8,128)} %self_hbm.1, s32[4]{0:T(128)} %offsets_hbm.1, f32[4]{0:T(128)} %strengths_hbm.1), custom_call_target="tpu_custom_call" | custom-call | tf_op jit(solution)/shard_map/pallas_call | solution.py:427
  55.6 2.1 %shard_map.78 = (f32[4,2,128,128]{3,2,1,0:T(8,128)}, f32[4,2,128,128]{3,2,1,0:T(8,128)}) custom-call(f32[4,2,128,128]{3,2,1,0:T(8,128)} %get-tuple-element.6.diag_ref, f32[4,2,128,128]{3,2,1,0:T(8,128)} %get-tuple-element.7.sigma_ref), custom_call_target="tpu_custom_call" | custom-call | tf_op jit(solution)/shard_map/pallas_call | solution.py:459

commit v6 on v5

--- a/solution.py
+++ b/solution.py
@@ -7,7 +7,6 @@
 
 OFFSET_MAX = 8
 
-PRECISE = lax.Precision.HIGHEST
 BROADENING = 0.2
 CONTACT_RATE = 0.5
 LEAD_WIDTH = 1.0
@@ -16,8 +15,16 @@
 HALF = 64
 
 
+def halves(x):
+    high = x.astype(jnp.bfloat16)
+    return high, (x - high.astype(jnp.float32)).astype(jnp.bfloat16)
+
+
 def dot(x, y):
-    return lax.dot_general(x, y, (((1,), (0,)), ((), ())), precision=PRECISE, preferred_element_type=jnp.float32)
+    once = lambda p, q: lax.dot_general(p, q, (((1,), (0,)), ((), ())), preferred_element_type=jnp.float32)
+    (x_high, x_low), (y_high, y_low) = halves(x), halves(y)
+    return once(x_high, y_high) + (once(x_high, y_low) + once(x_low, y_high))
+
 
 def packed_sign(shape):
     li = lax.broadcasted_iota(jnp.int32, shape, 1)

time: 58 us -> 53.5 us (0.922)
  the two profiles are of different devices: /device:TPU:29 before, /device:TPU:25 now
where the time goes in v6:
time: 53.5 us; the launch traced here: 53.3 us
  Pallas kernels  52.5 us (98%)
  between operations  0.8 us (1%)
    pallas_call x1, Pallas kernels, born(): pl.pallas_call(born_kernel, out_shape=(out, out), in_specs=[pl.BlockSpec(...  50.4 us
    pallas_call x1, Pallas kernels, write(): pl.pallas_call(write_kernel, out_shape=(shape, shape), in_specs=[pl.Block...  2.09 us

profile of v6, /device:TPU:25, one launch (start us, length us, event | category | flops | bytes accessed | tf_op | source)
XLA Modules:
  0.0 53.3 jit_solution(2283628374370855441)
XLA Ops:
  0.6 50.4 %shard_map.77 = (f32[4,2,128,128]{3,2,1,0:T(8,128)}, f32[4,2,128,128]{3,2,1,0:T(8,128)}) custom-call(s32[128]{0:T(128)} %owner_hbm.1, f32[1,2,128,128]{3,2,1,0:T(8,128)} %ham_hbm.1, f32[1,2,128,128]{3,2,1,0:T(8,128)} %link_hbm.1, f32[1,4,2,128,128]{4,3,2,1,0:T(8,128)} %self_hbm.1, s32[4]{0:T(128)} %offsets_hbm.1, f32[4]{0:T(128)} %strengths_hbm.1), custom_call_target="tpu_custom_call" | custom-call | tf_op jit(solution)/shard_map/pallas_call | solution.py:434
  51.1 2.1 %shard_map.78 = (f32[4,2,128,128]{3,2,1,0:T(8,128)}, f32[4,2,128,128]{3,2,1,0:T(8,128)}) custom-call(f32[4,2,128,128]{3,2,1,0:T(8,128)} %get-tuple-element.6.diag_ref, f32[4,2,128,128]{3,2,1,0:T(8,128)} %get-tuple-element.7.sigma_ref), custom_call_target="tpu_custom_call" | custom-call | tf_op jit(solution)/shard_map/pallas_call | solution.py:466

commit v7 on v6

--- a/solution.py
+++ b/solution.py
@@ -255,17 +255,9 @@
             v_copy(1, cell).wait_recv()
         return links[cell, 0], links[cell, 1]
 
-    def x_send(cell):
-        return remote(green_ref.at[cell], diag_ref.at[me], x_sent.at[cell], x_landed.at[me], {"cell": cell})
-
     def keep(cell, green):
         green_ref[cell, 0] = green[0]
         green_ref[cell, 1] = green[1]
-
-    def ship(cell):
-        @pl.when(me != cell)
-        def _():
-            x_send(cell).start()
 
     def x_copy(distance, slot):
         return remote(green_ref.at[other(distance)], diag_ref.at[slot], x_sent.at[distance - 1],
@@ -374,8 +366,8 @@
             for step in range(4):
                 weigh(q, o, step)
     solve(wait_a, wait_v, keep)
-    for cell in (1, 2, 0, 3):
-        ship(cell)
+    for distance in ARRIVALS:
+        x_copy(distance, me).start()
     send(0)
     diag_ref[me] = green_ref[me]
     receive_x(1)
@@ -393,10 +385,8 @@
     finish(3)
     stores.append(pltpu.make_async_copy(sigma_ref, sigma_out, stored.at[1]))
     stores[1].start()
-    for cell in range(4):
-        @pl.when(me != cell)
-        def _():
-            x_send(cell).wait_send()
+    for distance in ARRIVALS:
+        x_copy(distance, me).wait_send()
     for step in range(4):
         @pl.when(upper)
         def _():
@@ -442,7 +432,7 @@
             buffer(3), buffer(4), buffer(3), pltpu.VMEM(shape[1:], jnp.float32),
             buffer(4), pltpu.VMEM((4,) + shape, jnp.float32), pltpu.SMEM((4, 20), jnp.float32),
             dma((6,)), dma((3,)), dma((4,)), dma((3,)), dma((3,)),
-            dma((4,)), dma((4,)), dma((3, 4)), dma((4,)), dma((4, 4)), dma((2,)),
+            dma((3,)), dma((4,)), dma((3, 4)), dma((4,)), dma((4, 4)), dma((2,)),
         ],
         compiler_params=pltpu.CompilerParams(collective_id=0, has_side_effects=True),
     )(owner, hamiltonian, coupling, sigma_in, offsets, strengths)

time: 53.5 us -> 52.6 us (0.983)
  Pallas kernels: 52.5 us -> 51.4 us
    pallas_call x1, Pallas kernels: 50.4 us -> 49.3 us  [born(): pl.pallas_call(born_kernel, out_shape=(out, out), in_specs=[pl.BlockSpec(...]
where the time goes in v7:
time: 52.6 us; the launch traced here: 52.2 us
  Pallas kernels  51.4 us (98%)
  between operations  0.8 us (2%)
    pallas_call x1, Pallas kernels, born(): pl.pallas_call(born_kernel, out_shape=(out, out), in_specs=[pl.BlockSpec(...  49.3 us
    pallas_call x1, Pallas kernels, write(): pl.pallas_call(write_kernel, out_shape=(shape, shape), in_specs=[pl.Block...  2.09 us

profile of v7, /device:TPU:25, one launch (start us, length us, event | category | flops | bytes accessed | tf_op | source)
XLA Modules:
  0.0 52.2 jit_solution(18115155628211090043)
XLA Ops:
  0.6 49.3 %shard_map.77 = (f32[4,2,128,128]{3,2,1,0:T(8,128)}, f32[4,2,128,128]{3,2,1,0:T(8,128)}) custom-call(s32[128]{0:T(128)} %owner_hbm.1, f32[1,2,128,128]{3,2,1,0:T(8,128)} %ham_hbm.1, f32[1,2,128,128]{3,2,1,0:T(8,128)} %link_hbm.1, f32[1,4,2,128,128]{4,3,2,1,0:T(8,128)} %self_hbm.1, s32[4]{0:T(128)} %offsets_hbm.1, f32[4]{0:T(128)} %strengths_hbm.1), custom_call_target="tpu_custom_call" | custom-call | tf_op jit(solution)/shard_map/pallas_call | solution.py:424
  50.0 2.1 %shard_map.78 = (f32[4,2,128,128]{3,2,1,0:T(8,128)}, f32[4,2,128,128]{3,2,1,0:T(8,128)}) custom-call(f32[4,2,128,128]{3,2,1,0:T(8,128)} %get-tuple-element.6.diag_ref, f32[4,2,128,128]{3,2,1,0:T(8,128)} %get-tuple-element.7.sigma_ref), custom_call_target="tpu_custom_call" | custom-call | tf_op jit(solution)/shard_map/pallas_call | solution.py:456
